TPU v7x, 32 devices: a whole 2x2x4 slice. The times are simulated.
32 devices in a mesh: fsdp: 4 (over z), ctx: 2 (over core), tp: 4 (over y, x).
Axes of the slice: x: 2, y: 2, z: 4, core: 2. Of those that a mesh axis runs over, the one named last changes fastest.
Arguments:
- tokens: bfloat16 [6144, 2048], P(('fsdp', 'ctx')), may hold values from -6 to 6
- cotangent: bfloat16 [6144, 2048], P(('fsdp', 'ctx')), may hold values from -6 to 6
- adapter_ids: int32 [4, 5], replicated, may hold values from 0 to 7
- gain_attn: float32 [2048], replicated, may hold values from 0.5 to 1.5
- gain_mlp: float32 [2048], replicated, may hold values from 0.5 to 1.5
- query_weight: bfloat16 [2048, 2048], P('fsdp', 'tp'), may hold values from -0.125 to 0.125
- key_weight: bfloat16 [2048, 256], P('fsdp', 'tp'), may hold values from -0.125 to 0.125
- value_weight: bfloat16 [2048, 256], P('fsdp', 'tp'), may hold values from -0.125 to 0.125
- output_weight: bfloat16 [2048, 2048], P('tp', 'fsdp'), may hold values from -1 to 1
- gate_weight: bfloat16 [2048, 5632], P('fsdp', 'tp'), may hold values from -0.125 to 0.125
- up_weight: bfloat16 [2048, 5632], P('fsdp', 'tp'), may hold values from -0.125 to 0.125
- down_weight: bfloat16 [5632, 2048], P('tp', 'fsdp'), may hold values from -0.078125 to 0.078125
- query_first: bfloat16 [8, 2048, 16], replicated, may hold values from -0.125 to 0.125
- query_second: bfloat16 [8, 16, 2048], P(None, None, 'tp'), may hold values from -1.5 to 1.5
- key_first: bfloat16 [8, 2048, 16], replicated, may hold values from -0.125 to 0.125
- key_second: bfloat16 [8, 16, 256], P(None, None, 'tp'), may hold values from -1.5 to 1.5
- value_first: bfloat16 [8, 2048, 16], replicated, may hold values from -0.125 to 0.125
- value_second: bfloat16 [8, 16, 256], P(None, None, 'tp'), may hold values from -1.5 to 1.5
- output_first: bfloat16 [8, 2048, 16], P(None, 'tp'), may hold values from -1 to 1
- output_second: bfloat16 [8, 16, 2048], replicated, may hold values from -1.5 to 1.5
- gate_first: bfloat16 [8, 2048, 16], replicated, may hold values from -0.125 to 0.125
- gate_second: bfloat16 [8, 16, 5632], P(None, None, 'tp'), may hold values from -1.5 to 1.5
- up_first: bfloat16 [8, 2048, 16], replicated, may hold values from -0.125 to 0.125
- up_second: bfloat16 [8, 16, 5632], P(None, None, 'tp'), may hold values from -1.5 to 1.5
- down_first: bfloat16 [8, 5632, 16], P(None, 'tp'), may hold values from -0.078125 to 0.078125
- down_second: bfloat16 [8, 16, 2048], replicated, may hold values from -1.5 to 1.5
Outputs:
- output: bfloat16 [6144, 2048], P(('fsdp', 'ctx'))
- input_grad: float32 [6144, 2048], P(('fsdp', 'ctx'))
- query_first_grad: float32 [8, 2048, 16], replicated
- query_second_grad: float32 [8, 16, 2048], P(None, None, 'tp')
- key_first_grad: float32 [8, 2048, 16], replicated
- key_second_grad: float32 [8, 16, 256], P(None, None, 'tp')
- value_first_grad: float32 [8, 2048, 16], replicated
- value_second_grad: float32 [8, 16, 256], P(None, None, 'tp')
- output_first_grad: float32 [8, 2048, 16], P(None, 'tp')
- output_second_grad: float32 [8, 16, 2048], replicated
- gate_first_grad: float32 [8, 2048, 16], replicated
- gate_second_grad: float32 [8, 16, 5632], P(None, None, 'tp')
- up_first_grad: float32 [8, 2048, 16], replicated
- up_second_grad: float32 [8, 16, 5632], P(None, None, 'tp')
- down_first_grad: float32 [8, 5632, 16], P(None, 'tp')
- down_second_grad: float32 [8, 16, 2048], replicated
All inputs are finite; a program needn't handle non-finite values.
Results may differ from a plain program's by a relative error of at most 0.019.
The roundings to bfloat16 on the way count: a program that leaves them out, or rounds other values in their place, can miss the bound.
Values may be sent and summed in bfloat16 or wider, within the bound.
No kernel may reach another device: no remote copies, remote signals or barrier semaphores. Data moves between devices by JAX's collectives and lax.ppermute only.
A program may use at most 112 MiB of HBM per device.

v0:
```python
import jax
import jax.numpy as jnp
from jax import lax
from jax.sharding import PartitionSpec as P

HD = 64
RANK = 16
ADAPTERS = 8
PROMPT = 1024
CONT_LEN = 128
GROUP = 1536


EPS = 1e-05
SCALE = 0.125
THETA = 10000.0


def times(left, right):
    return jnp.dot(left, right, preferred_element_type=jnp.float32)


def times_transposed(left, right):
    return lax.dot_general(
        left, right, (((1,), (1,)), ((), ())), preferred_element_type=jnp.float32
    )


def inner_left(left, right):
    return lax.dot_general(
        left, right, (((0,), (0,)), ((), ())), preferred_element_type=jnp.float32
    )


def layout(stream):
    in_prompt = stream < PROMPT
    later = jnp.maximum(stream - PROMPT, 0)
    sequence = jnp.where(in_prompt, 0, 1 + later // CONT_LEN)
    position = jnp.where(in_prompt, stream, PROMPT + later % CONT_LEN)
    return (sequence, position)


def selector(sequence, row_ids):
    places = jnp.arange(row_ids.shape[0], dtype=jnp.int32)
    chosen = jnp.sum(jnp.where(sequence[:, None] == places[None, :], row_ids[None, :], 0), axis=1)
    columns = jnp.arange(ADAPTERS * RANK, dtype=jnp.int32) // RANK
    return (chosen[:, None] == columns[None, :]).astype(jnp.float32)


def angles(position):
    freqs = THETA ** (-(jnp.arange(HD // 2, dtype=jnp.int32) * 2).astype(jnp.float32) / HD)
    turned = position.astype(jnp.float32)[:, None] * freqs[None, :]
    return (jnp.cos(turned), jnp.sin(turned))


def rotate(values, cosine, sine):
    half = values.shape[-1] // 2
    first = values[..., :half]
    second = values[..., half:]
    return jnp.concatenate(
        [first * cosine - second * sine, second * cosine + first * sine], axis=-1
    )


def flat_first(first):
    return jnp.transpose(first, (1, 0, 2)).reshape(first.shape[1], first.shape[0] * first.shape[2])


def flat_second(second):
    return second.reshape(second.shape[0] * second.shape[1], second.shape[2])


def unflat_first(grad, first):
    return jnp.transpose(grad.reshape(first.shape[1], first.shape[0], first.shape[2]), (1, 0, 2))


def unflat_second(grad, second):
    return grad.reshape(second.shape)


def rms_back(values, scaling, gain, grad_normed):
    weighted = grad_normed * gain
    return scaling * weighted - values * scaling * scaling * scaling * jnp.mean(
        weighted * values, axis=1, keepdims=True
    )


def shards(
    tokens,
    cotangent,
    adapter_ids,
    gain_attn,
    gain_mlp,
    query_weight,
    key_weight,
    value_weight,
    output_weight,
    gate_weight,
    up_weight,
    down_weight,
    query_first,
    query_second,
    key_first,
    key_second,
    value_first,
    value_second,
    output_first,
    output_second,
    gate_first,
    gate_second,
    up_first,
    up_second,
    down_first,
    down_second,
):
    rows = tokens.shape[0]
    heads = query_weight.shape[1] // HD
    kv_heads = key_weight.shape[1] // HD
    ratio = heads // kv_heads
    stream = lax.axis_index("ctx") * rows + jnp.arange(rows, dtype=jnp.int32)
    whole_stream = jnp.arange(GROUP, dtype=jnp.int32)
    sequence, position = layout(stream)
    whole_sequence, whole_position = layout(whole_stream)
    row_ids = lax.dynamic_index_in_dim(adapter_ids, lax.axis_index("fsdp"), 0, False)
    select = selector(sequence, row_ids)
    select_low = select.astype(jnp.bfloat16)
    cosine, sine = angles(position)
    allowed = (whole_stream[None, :] <= stream[:, None]) & (
        (whole_stream[None, :] < PROMPT) | (whole_sequence[None, :] == sequence[:, None])
    )
    frozen_local = (
        query_weight,
        key_weight,
        value_weight,
        output_weight,
        gate_weight,
        up_weight,
        down_weight,
    )
    gathered = (
        lax.all_gather(frozen_local[0], "fsdp", axis=0, tiled=True),
        lax.all_gather(frozen_local[1], "fsdp", axis=0, tiled=True),
        lax.all_gather(frozen_local[2], "fsdp", axis=0, tiled=True),
        lax.all_gather(frozen_local[3], "fsdp", axis=1, tiled=True),
        lax.all_gather(frozen_local[4], "fsdp", axis=0, tiled=True),
        lax.all_gather(frozen_local[5], "fsdp", axis=0, tiled=True),
        lax.all_gather(frozen_local[6], "fsdp", axis=1, tiled=True),
    )
    query_full, key_full, value_full, output_full, gate_full, up_full, down_full = gathered

    def inner(source, first):
        return (times(source, flat_first(first)) * select).astype(jnp.bfloat16)

    source = tokens.astype(jnp.float32)
    scale_one = lax.rsqrt(jnp.mean(source * source, axis=1, keepdims=True) + EPS)
    normed = (source * scale_one * gain_attn).astype(jnp.bfloat16)
    query_inner = inner(normed, query_first)
    key_inner = inner(normed, key_first)
    value_inner = inner(normed, value_first)
    query = times(normed, query_full) + times(query_inner, flat_second(query_second))
    key = times(normed, key_full) + times(key_inner, flat_second(key_second))
    value = times(normed, value_full) + times(value_inner, flat_second(value_second))
    query_rot = rotate(query.reshape(rows, heads, HD), cosine[:, None, :], sine[:, None, :]).astype(
        jnp.bfloat16
    )
    key_rot = rotate(key.reshape(rows, kv_heads, HD), cosine[:, None, :], sine[:, None, :]).astype(
        jnp.bfloat16
    )
    kv_local = jnp.concatenate(
        [key_rot.reshape(rows, kv_heads * HD), value.astype(jnp.bfloat16)], axis=1
    )
    kv_whole = lax.all_gather(kv_local, "ctx", axis=0, tiled=True)
    key_stack = jnp.transpose(kv_whole[:, : kv_heads * HD].reshape(GROUP, kv_heads, HD), (1, 0, 2))
    value_stack = jnp.transpose(
        kv_whole[:, kv_heads * HD :].reshape(GROUP, kv_heads, HD), (1, 0, 2)
    )
    query_heads = jnp.transpose(query_rot, (1, 0, 2))
    head_index = jnp.arange(heads, dtype=jnp.int32)

    def scores_of(query_one, key_one):
        return jnp.where(allowed, times_transposed(query_one, key_one) * SCALE, -1e30)

    def attend(item):
        query_one, index = item
        key_one = lax.dynamic_index_in_dim(key_stack, index // ratio, 0, False)
        value_one = lax.dynamic_index_in_dim(value_stack, index // ratio, 0, False)
        scores = scores_of(query_one, key_one)
        largest = jnp.max(scores, axis=1, keepdims=True)
        expo = jnp.exp(scores - largest)
        total = jnp.sum(expo, axis=1, keepdims=True)
        probs = (expo / total).astype(jnp.bfloat16)
        return (times(probs, value_one), (largest + jnp.log(total))[:, 0])

    attended, log_total = lax.map(attend, (query_heads, head_index))
    att_low = jnp.transpose(attended, (1, 0, 2)).reshape(rows, heads * HD).astype(jnp.bfloat16)
    out_part = times(att_low, flat_first(output_first)) * select
    out_main, out_inner = lax.psum((times(att_low, output_full), out_part), "tp")
    out_inner_low = out_inner.astype(jnp.bfloat16)
    middle = source + out_main + times(out_inner_low, flat_second(output_second))
    scale_two = lax.rsqrt(jnp.mean(middle * middle, axis=1, keepdims=True) + EPS)
    normed_two = (middle * scale_two * gain_mlp).astype(jnp.bfloat16)
    gate_inner = inner(normed_two, gate_first)
    up_inner = inner(normed_two, up_first)
    gate = times(normed_two, gate_full) + times(gate_inner, flat_second(gate_second))
    upper = times(normed_two, up_full) + times(up_inner, flat_second(up_second))
    sigmoid_gate = jax.nn.sigmoid(gate)
    swish = gate * sigmoid_gate
    hidden = (swish * upper).astype(jnp.bfloat16)
    down_part = times(hidden, flat_first(down_first)) * select
    down_main, down_inner = lax.psum((times(hidden, down_full), down_part), "tp")
    down_inner_low = down_inner.astype(jnp.bfloat16)
    result = middle + down_main + times(down_inner_low, flat_second(down_second))
    output = result.astype(jnp.bfloat16)
    regathered = (
        lax.all_gather(frozen_local[0], "fsdp", axis=0, tiled=True),
        lax.all_gather(frozen_local[1], "fsdp", axis=0, tiled=True),
        lax.all_gather(frozen_local[2], "fsdp", axis=0, tiled=True),
        lax.all_gather(frozen_local[3], "fsdp", axis=1, tiled=True),
        lax.all_gather(frozen_local[4], "fsdp", axis=0, tiled=True),
        lax.all_gather(frozen_local[5], "fsdp", axis=0, tiled=True),
        lax.all_gather(frozen_local[6], "fsdp", axis=1, tiled=True),
    )
    query_full, key_full, value_full, output_full, gate_full, up_full, down_full = regathered
    upstream = cotangent.astype(jnp.float32)
    grad_down_second = inner_left(down_inner_low, cotangent)
    grad_down_inner = (
        times_transposed(cotangent, flat_second(down_second)).astype(jnp.bfloat16) * select_low
    )
    grad_hidden = times_transposed(cotangent, down_full) + times_transposed(
        grad_down_inner, flat_first(down_first)
    )
    grad_down_first = inner_left(hidden, grad_down_inner)
    grad_gate = (grad_hidden * upper * (sigmoid_gate * (1.0 + gate * (1.0 - sigmoid_gate)))).astype(
        jnp.bfloat16
    )
    grad_upper = (grad_hidden * swish).astype(jnp.bfloat16)
    grad_gate_second = inner_left(gate_inner, grad_gate)
    grad_up_second = inner_left(up_inner, grad_upper)
    part_normed_two, part_gate, part_up = lax.psum(
        (
            times_transposed(grad_gate, gate_full) + times_transposed(grad_upper, up_full),
            times_transposed(grad_gate, flat_second(gate_second)),
            times_transposed(grad_upper, flat_second(up_second)),
        ),
        "tp",
    )
    grad_gate_inner = part_gate.astype(jnp.bfloat16) * select_low
    grad_up_inner = part_up.astype(jnp.bfloat16) * select_low
    grad_gate_first = inner_left(normed_two, grad_gate_inner)
    grad_up_first = inner_left(normed_two, grad_up_inner)
    grad_normed_two = (
        part_normed_two
        + times_transposed(grad_gate_inner, flat_first(gate_first))
        + times_transposed(grad_up_inner, flat_first(up_first))
    )
    grad_middle = upstream + rms_back(middle, scale_two, gain_mlp, grad_normed_two)
    grad_branch = grad_middle.astype(jnp.bfloat16)
    grad_output_second = inner_left(out_inner_low, grad_branch)
    grad_out_inner = (
        times_transposed(grad_branch, flat_second(output_second)).astype(jnp.bfloat16) * select_low
    )
    grad_att = (
        times_transposed(grad_branch, output_full)
        + times_transposed(grad_out_inner, flat_first(output_first))
    ).astype(jnp.bfloat16)
    grad_output_first = inner_left(att_low, grad_out_inner)
    grad_heads = jnp.transpose(grad_att.reshape(rows, heads, HD), (1, 0, 2))

    def back_head(carry, item):
        query_one, grad_one, total_one, index = item
        kv_index = index // ratio
        key_one = lax.dynamic_index_in_dim(key_stack, kv_index, 0, False)
        value_one = lax.dynamic_index_in_dim(value_stack, kv_index, 0, False)
        probs = jnp.exp(scores_of(query_one, key_one) - total_one[:, None])
        grad_probs = times_transposed(grad_one, value_one)
        delta = jnp.sum(probs * grad_probs, axis=1, keepdims=True)
        grad_scores = (probs * (grad_probs - delta)).astype(jnp.bfloat16)
        grad_query = times(grad_scores, key_one) * SCALE
        grad_key = inner_left(grad_scores, query_one) * SCALE
        grad_value = inner_left(probs.astype(jnp.bfloat16), grad_one)
        key_acc, value_acc = carry
        key_acc = lax.dynamic_update_index_in_dim(
            key_acc, lax.dynamic_index_in_dim(key_acc, kv_index, 0, False) + grad_key, kv_index, 0
        )
        value_acc = lax.dynamic_update_index_in_dim(
            value_acc,
            lax.dynamic_index_in_dim(value_acc, kv_index, 0, False) + grad_value,
            kv_index,
            0,
        )
        return ((key_acc, value_acc), grad_query)

    empty = jnp.zeros((kv_heads, GROUP, HD), jnp.float32)
    (key_acc, value_acc), grad_query_heads = lax.scan(
        back_head, (empty, empty), (query_heads, grad_heads, log_total, head_index)
    )
    kv_grad_whole = jnp.concatenate(
        [
            jnp.transpose(key_acc, (1, 0, 2)).reshape(GROUP, kv_heads * HD),
            jnp.transpose(value_acc, (1, 0, 2)).reshape(GROUP, kv_heads * HD),
        ],
        axis=1,
    )
    kv_grad_local = lax.psum_scatter(kv_grad_whole, "ctx", scatter_dimension=0, tiled=True)
    grad_key_rot = kv_grad_local[:, : kv_heads * HD].reshape(rows, kv_heads, HD)
    grad_value_low = kv_grad_local[:, kv_heads * HD :].astype(jnp.bfloat16)
    grad_query_low = (
        rotate(jnp.transpose(grad_query_heads, (1, 0, 2)), cosine[:, None, :], -sine[:, None, :])
        .reshape(rows, heads * HD)
        .astype(jnp.bfloat16)
    )
    grad_key_low = (
        rotate(grad_key_rot, cosine[:, None, :], -sine[:, None, :])
        .reshape(rows, kv_heads * HD)
        .astype(jnp.bfloat16)
    )
    grad_query_second = inner_left(query_inner, grad_query_low)
    grad_key_second = inner_left(key_inner, grad_key_low)
    grad_value_second = inner_left(value_inner, grad_value_low)
    part_normed, part_query, part_key, part_value = lax.psum(
        (
            times_transposed(grad_query_low, query_full)
            + times_transposed(grad_key_low, key_full)
            + times_transposed(grad_value_low, value_full),
            times_transposed(grad_query_low, flat_second(query_second)),
            times_transposed(grad_key_low, flat_second(key_second)),
            times_transposed(grad_value_low, flat_second(value_second)),
        ),
        "tp",
    )
    grad_query_inner = part_query.astype(jnp.bfloat16) * select_low
    grad_key_inner = part_key.astype(jnp.bfloat16) * select_low
    grad_value_inner = part_value.astype(jnp.bfloat16) * select_low
    grad_query_first = inner_left(normed, grad_query_inner)
    grad_key_first = inner_left(normed, grad_key_inner)
    grad_value_first = inner_left(normed, grad_value_inner)
    grad_normed = (
        part_normed
        + times_transposed(grad_query_inner, flat_first(query_first))
        + times_transposed(grad_key_inner, flat_first(key_first))
        + times_transposed(grad_value_inner, flat_first(value_first))
    )
    input_grad = grad_middle + rms_back(source, scale_one, gain_attn, grad_normed)
    summed = lax.psum(
        (
            unflat_first(grad_query_first, query_first),
            unflat_second(grad_query_second, query_second),
            unflat_first(grad_key_first, key_first),
            unflat_second(grad_key_second, key_second),
            unflat_first(grad_value_first, value_first),
            unflat_second(grad_value_second, value_second),
            unflat_first(grad_output_first, output_first),
            unflat_second(grad_output_second, output_second),
            unflat_first(grad_gate_first, gate_first),
            unflat_second(grad_gate_second, gate_second),
            unflat_first(grad_up_first, up_first),
            unflat_second(grad_up_second, up_second),
            unflat_first(grad_down_first, down_first),
            unflat_second(grad_down_second, down_second),
        ),
        ("fsdp", "ctx"),
    )
    return (output, input_grad) + tuple(summed)


def solution(mesh):
    placed = (
        P(("fsdp", "ctx"), None),
        P(("fsdp", "ctx"), None),
        P(),
        P(),
        P(),
        P("fsdp", "tp"),
        P("fsdp", "tp"),
        P("fsdp", "tp"),
        P("tp", "fsdp"),
        P("fsdp", "tp"),
        P("fsdp", "tp"),
        P("tp", "fsdp"),
        P(),
        P(None, None, "tp"),
        P(),
        P(None, None, "tp"),
        P(),
        P(None, None, "tp"),
        P(None, "tp", None),
        P(),
        P(),
        P(None, None, "tp"),
        P(),
        P(None, None, "tp"),
        P(None, "tp", None),
        P(),
    )
    return jax.shard_map(
        shards,
        mesh=mesh,
        in_specs=placed,
        out_specs=(
            P(("fsdp", "ctx"), None),
            P(("fsdp", "ctx"), None),
            P(),
            P(None, None, "tp"),
            P(),
            P(None, None, "tp"),
            P(),
            P(None, None, "tp"),
            P(None, "tp", None),
            P(),
            P(),
            P(None, None, "tp"),
            P(),
            P(None, None, "tp"),
            P(None, "tp", None),
            P(),
        ),
        check_vma=False,
    )
```

profile of v0, /device:TPU:0, one launch (start us, length us, event | category | flops | bytes accessed | tf_op | source)
XLA Modules:
  0.0 1468.6 jit_solution(8692617448938960585)
XLA Ops:
  12.4 16.8 %all_gather.33 = bf16[2048,64]{0,1:T(8,128)(2,1)S(1)} all-gather(bf16[512,64]{0,1:T(8,128)(2,1)S(1)} %copy-done.82), channel_id=1, replica_groups=mesh['fsdp'=4,'ctx'=2,'tp'=4] {'fsdp'}, dimensions={0}, use_global_device_ids=true | all-gather | bytes 327680 | tf_op jit(solution)/shard_map/all_gather | solution.py:143
  34.3 16.5 %all_gather.32 = bf16[2048,64]{0,1:T(8,128)(2,1)S(1)} all-gather(bf16[512,64]{0,1:T(8,128)(2,1)S(1)} %copy-done.83), channel_id=1, replica_groups=mesh['fsdp'=4,'ctx'=2,'tp'=4] {'fsdp'}, dimensions={0}, use_global_device_ids=true | all-gather | bytes 327680 | tf_op jit(solution)/shard_map/all_gather | solution.py:142
  64.3 4.4 fusion.157
  71.0 52.2 %while.32 = (s32[]{:T(128)}, bf16[8,768,64]{1,2,0:T(8,128)(2,1)S(1)}, f32[8,768]{1,0:T(8,128)}, bf16[8,768,64]{2,1,0:T(8,128)(2,1)}, bf16[1,1536,64]{2,1,0:T(8,1...) while((s32[]{:T(128)}, ...), condition=%wide.region_5.6_spmd.clone.clone, body=%wide.region_2.5_spmd.clone.sunk.clone | while | flops 316144896 | bytes 15191673 | solution.py:194
  71.0 3.2 fusion.302
  123.3 6.4 fusion.162
  130.9 3.7 fusion.57
  135.0 23.9 %all-reduce.23 = bf16[768,128]{0,1:T(8,128)(2,1)S(1)} all-reduce(f32[768,128]{0,1:T(8,128)S(1)} %convolution_select_fusion.3), channel_id=1, replica_groups=mesh['fsdp'=4,'ctx'=2,'tp'=4] {'tp'}, use_global_device_ids=true, to_apply=%region_7.8 | all-reduce | flops 98304 | bytes 589824 | tf_op jit(solution)/shard_map/psum | solution.py:197
  158.8 59.2 %all-gather.14.cloned.1.call-done = bf16[1408,2048]{1,0:T(8,128)(2,1)} async-done(((bf16[1408,512]{1,0:T(8,128)(2,1)}), bf16[1408,2048]{1,0:T(8,128)(2,1)}) %all-gather.14.cloned.1.call-update) | async-done | bytes 5767184 | tf_op jit(solution)/shard_map/all_gather | solution.py:147
  218.0 9.8 fusion.166
  227.8 130.7 %all-reduce.14.cloned.1.call-done = f32[768,2048]{1,0:T(8,128)} async-done(((f32[768,2048]{1,0:T(8,128)}), f32[768,2048]{1,0:T(8,128)}) %all-reduce.14.cloned.1.call-update) | async-done | bytes 6291472 | tf_op jit(solution)/shard_map/psum | solution.py:197
  358.5 5.1 multiply_reduce_fusion.2
  369.1 97.6 %all-gather.10.cloned.1.call-done = bf16[2048,1408]{1,0:T(8,128)(2,1)} async-done(((bf16[512,1408]{1,0:T(8,128)(2,1)}), bf16[2048,1408]{1,0:T(8,128)(2,1)}) %all-gather.10.cloned.1.call-update) | async-done | bytes 5767184 | tf_op jit(solution)/shard_map/all_gather | solution.py:145
  466.6 8.4 fusion.163
  477.9 95.2 %all-gather.12.cloned.1.call-done = bf16[2048,1408]{1,0:T(8,128)(2,1)} async-done(((bf16[512,1408]{1,0:T(8,128)(2,1)}), bf16[2048,1408]{1,0:T(8,128)(2,1)}) %all-gather.12.cloned.1.call-update) | async-done | bytes 5767184 | tf_op jit(solution)/shard_map/all_gather | solution.py:146
  573.1 8.4 fusion.164
  583.9 5.9 multiply_convert_fusion.2
  589.8 5.1 fusion.167
  595.0 7.1 convolution_add_fusion.3
  607.1 59.4 %all-reduce.24 = (bf16[768,128]{0,1:T(8,128)(2,1)S(1)}, bf16[768,128]{0,1:T(8,128)(2,1)S(1)}) all-reduce(f32[768,128]{0,1:T(8,128)S(1)} %fusion.168, f32[768,128]{0,1:T(8,128)S(1)} %fusion.169), channel_id=1, replica_groups=mesh['fsdp'=4,'ctx'=2,'tp'=4] {'tp'}, use_global_device_ids=true, to_apply=%region_12.13 | all-reduce | flops 196608 | bytes 1179648 | tf_op jit(solution)/shard_map/psum | solution.py:239
  666.5 3.7 fusion.140
  670.2 93.9 %all-reduce.16.cloned.1.call-done = f32[768,2048]{1,0:T(8,128)} async-done(((f32[768,2048]{1,0:T(8,128)}), f32[768,2048]{1,0:T(8,128)}) %all-reduce.16.cloned.1.call-update) | async-done | bytes 6291472 | tf_op jit(solution)/shard_map/psum | solution.py:239
  764.1 8.4 multiply_reduce_fusion.1
  783.5 76.2 %while.33 = (s32[]{:T(128)}, f32[1,1536,64]{1,2,0:T(8,128)S(1)}, f32[1,1536,64]{1,2,0:T(8,128)S(1)}, f32[8,768,64]{1,2,0:T(8,128)}, bf16[8,768,64]{2,1,0:T(8,128...) while((s32[]{:T(128)}, f32[1,1536,64]{1,2,0:T(8,128)S(1)}, ...), condition=%wide.region_17.18_spmd.clone.clone, body=%wide.region_15.17_spmd.clone.sunk.clone | while | flops 770653440 | bytes 38761116 | solution.py:294
  785.1 3.8 multiply_reduce_fusion.5
  794.6 3.8 multiply_reduce_fusion.5
  804.2 3.8 multiply_reduce_fusion.5
  813.7 3.8 multiply_reduce_fusion.5
  823.2 3.8 multiply_reduce_fusion.5
  832.7 3.8 multiply_reduce_fusion.5
  842.3 3.8 multiply_reduce_fusion.5
  851.8 3.8 multiply_reduce_fusion.5
  860.8 9.7 fusion.165
  872.1 4.4 fusion.170
  880.0 3.6 add_add_fusion
  883.7 3.3 convolution_select_fusion.4
  887.0 3.2 fusion.172
  900.8 109.5 %all-reduce.25 = (bf16[768,128]{0,1:T(8,128)(2,1)S(1)}, bf16[768,128]{0,1:T(8,128)(2,1)S(1)}, bf16[768,128]{0,1:T(8,128)(2,1)S(1)}, bf16[768,128]{0,1:T(8,128)(2,1)S(1)}) all-reduce(f32[768,128]{0,1:T(8,128)S(1)} %copy-done.72, f32[768,128]{0,1:T(8,128)S(1)} %fusion.112, ...), channel_id=1, replica_groups=mesh['fsdp'=4,'ctx'=2,'tp'=4] {'tp'}, use_global_device_ids=true, to_apply=%region_10.11 | all-reduce | flops 393216 | bytes 2359296 | tf_op jit(solution)/shard_map/psum | solution.py:210
  1012.0 3.7 fusion.145
  1015.6 4.4 fusion.149
  1021.7 3.4 fusion.176
  1026.2 3.7 fusion.151
  1029.9 3.7 fusion.147
  1033.6 140.9 %all-reduce.22.cloned.1.call-done = (f32[768,2048]{1,0:T(8,128)}, f32[768,2048]{1,0:T(8,128)}) async-done(((f32[768,2048]{1,0:T(8,128)}, f32[768,2048]{1,0:T(8,128)}), (f32[768,2048]{1,0:T(8,128)}, f32[768,2048]{1,0:T(8,128)})) %all-reduce.22.cloned.1.call-update) | async-done | bytes 12582928 | tf_op jit(solution)/shard_map/psum | solution.py:210
  1174.5 8.7 fusion.52
  1189.6 3.9 fusion.49
  1193.5 38.3 %all-reduce.18.cloned.1.call-done = (f32[8,16,64]{2,1,0:T(8,128)}, f32[8,16,64]{2,1,0:T(8,128)}) async-done(((f32[8,16,64]{2,1,0:T(8,128)}, f32[8,16,64]{2,1,0:T(8,128)}), (f32[8,16,64]{2,1,0:T(8,128)}, f32[8,16,64]{2,1,0:T(8,128)})) %all-reduce.18.cloned.1.call-update) | async-done | bytes 65552 | tf_op jit(solution)/shard_map/psum | solution.py:344
  1231.8 214.1 %all-reduce.20.cloned.1.call-done = (f32[8,2048,16]{1,2,0:T(8,128)}, f32[8,16,512]{2,1,0:T(8,128)}, f32[8,2048,16]{1,2,0:T(8,128)}, f32[8,2048,16]{1,2,0:T(8,128...) async-done(((f32[8,2048,16]{1,2,0:T(8,128)}, ...) | async-done | bytes 10027024 | tf_op jit(solution)/shard_map/psum | solution.py:344
  (433 shorter events, 191.3 us)
Async XLA Ops:
  7.2 351.3 %copy-start = (bf16[8,16,2048]{2,1,0:T(8,128)(2,1)S(1)}, bf16[8,16,2048]{2,1,0:T(8,128)(2,1)}, u32[]{:S(2)}) copy-start(bf16[8,16,2048]{2,1,0:T(8,128)(2,1)} %param.49) | copy-start | bytes 1572868
  7.2 22.0 %copy-start.89 = (f32[2048]{0:T(1024)S(1)}, f32[2048]{0:T(1024)}, u32[]{:S(2)}) copy-start(f32[2048]{0:T(1024)} %param.33) | copy-start | bytes 24580
  7.2 57.1 %all-gather.6.cloned.1.call-start = ((), (), s32[]{:S(2)}) async-start(), calls=%async_computation.1 | async-start | bytes 2621440 | tf_op jit(solution)/shard_map/all_gather | solution.py:141
  8.0 115.3 %all-gather.8.cloned.1.call-start = ((), (), s32[]{:S(2)}) async-start(), calls=%async_computation.2 | async-start | bytes 2621440 | tf_op jit(solution)/shard_map/all_gather | solution.py:144
  8.7 209.3 %all-gather.14.cloned.1.call-start = ((), (), s32[]{:S(2)}) async-start(), calls=%async_computation.6 | async-start | bytes 7208960 | tf_op jit(solution)/shard_map/all_gather | solution.py:147
  9.4 349.0 %all-reduce.14.cloned.1.call-start = ((), (), s32[]{:S(2)}) async-start(), calls=%async_computation.3 | async-start | bytes 12582912 | tf_op jit(solution)/shard_map/psum | solution.py:197
  9.6 49.6 %copy-start.91 = (f32[32]{0:T(128)}, f32[32]{0:T(128)S(1)}, u32[]{:S(2)}) copy-start(f32[32]{0:T(128)S(1)} %multiply_power_fusion) | copy-start | bytes 388
  9.6 49.6 %copy-start.80 = (f32[768]{0:T(1024)}, f32[768]{0:T(1024)S(1)}, u32[]{:S(2)}) copy-start(f32[768]{0:T(1024)S(1)} %fusion.119) | copy-start | bytes 9220
  9.7 22.3 %copy-start.62 = (bf16[8,2048,16]{1,2,0:T(8,128)(2,1)S(1)}, bf16[8,2048,16]{1,2,0:T(8,128)(2,1)}, u32[]{:S(2)}) copy-start(bf16[8,2048,16]{1,2,0:T(8,128)(2,1)} %param.42) | copy-start | bytes 1572868
  12.3 20.9 %copy-start.86 = (f32[768]{0:T(1024)}, f32[768]{0:T(1024)S(1)}, u32[]{:S(2)}) copy-start(f32[768]{0:T(1024)S(1)} %add_rsqrt_fusion.1) | copy-start | bytes 9220
  32.0 20.6 %copy-start.3 = (bf16[768,2048]{1,0:T(8,128)(2,1)}, bf16[768,2048]{1,0:T(8,128)(2,1)S(1)}, u32[]{:S(2)}) copy-start(bf16[768,2048]{1,0:T(8,128)(2,1)S(1)} %fusion.45) | copy-start | bytes 9437188
  33.2 19.4 %copy-start.60 = (bf16[8,2048,16]{1,2,0:T(8,128)(2,1)S(1)}, bf16[8,2048,16]{1,2,0:T(8,128)(2,1)}, u32[]{:S(2)}) copy-start(bf16[8,2048,16]{1,2,0:T(8,128)(2,1)} %param.44) | copy-start | bytes 1572868
  55.8 13.3 copy-start.37
  58.9 9.8 copy-start.43
  123.2 11.4 copy-start.10
  129.7 337.0 %all-gather.10.cloned.1.call-start = ((), (), s32[]{:S(2)}) async-start(), calls=%async_computation.4 | async-start | bytes 7208960 | tf_op jit(solution)/shard_map/all_gather | solution.py:145
  130.3 442.8 %all-gather.12.cloned.1.call-start = ((), (), s32[]{:S(2)}) async-start(), calls=%async_computation.5 | async-start | bytes 7208960 | tf_op jit(solution)/shard_map/all_gather | solution.py:146
  130.9 633.2 %all-reduce.16.cloned.1.call-start = ((), (), s32[]{:S(2)}) async-start(), calls=%async_computation.7 | async-start | bytes 12582912 | tf_op jit(solution)/shard_map/psum | solution.py:239
  158.8 199.7 %copy-start.23 = (bf16[768,128]{0,1:T(8,128)(2,1)}, bf16[768,128]{0,1:T(8,128)(2,1)S(1)}, u32[]{:S(2)}) copy-start(bf16[768,128]{0,1:T(8,128)(2,1)S(1)} %all-reduce.23) | copy-start | bytes 589828
  367.5 107.6 %copy-start.47 = (bf16[768,128]{0,1:T(8,128)(2,1)}, bf16[768,128]{0,1:T(8,128)(2,1)S(1)}, u32[]{:S(2)}) copy-start(bf16[768,128]{0,1:T(8,128)(2,1)S(1)} %fusion.55) | copy-start | bytes 589828
  369.1 212.5 %copy-start.45 = (bf16[768,128]{0,1:T(8,128)(2,1)}, bf16[768,128]{0,1:T(8,128)(2,1)S(1)}, u32[]{:S(2)}) copy-start(bf16[768,128]{0,1:T(8,128)(2,1)S(1)} %fusion.56) | copy-start | bytes 589828
  369.1 106.0 %copy-start.28 = (bf16[8,16,1408]{2,1,0:T(8,128)(2,1)S(1)}, bf16[8,16,1408]{2,1,0:T(8,128)(2,1)}, u32[]{:S(2)}) copy-start(bf16[8,16,1408]{2,1,0:T(8,128)(2,1)} %param.51) | copy-start | bytes 1081348
  477.9 103.6 %copy-start.29 = (bf16[8,16,1408]{2,1,0:T(8,128)(2,1)S(1)}, bf16[8,16,1408]{2,1,0:T(8,128)(2,1)}, u32[]{:S(2)}) copy-start(bf16[8,16,1408]{2,1,0:T(8,128)(2,1)} %param.53) | copy-start | bytes 1081348
  583.9 11.0 slice-start.14
  602.0 274.5 %reduce-scatter.2.cloned.1.call-start = ((), (), s32[]{:S(2)}) async-start(), calls=%async_computation.8 | async-start | bytes 1179648 | tf_op jit(solution)/shard_map/reduce_scatter | solution.py:304
  666.5 97.6 %copy-start.39 = (bf16[768,128]{0,1:T(8,128)(2,1)}, bf16[768,128]{0,1:T(8,128)(2,1)S(1)}, u32[]{:S(2)}) copy-start(bf16[768,128]{0,1:T(8,128)(2,1)S(1)} %get-tuple-element.347) | copy-start | bytes 589828
  764.1 8.4 slice-start.1
  764.1 9.3 copy-start.9
  860.7 313.7 %all-reduce.22.cloned.1.call-start = ((), (), s32[]{:S(2)}) async-start(), calls=%async_computation.11 | async-start | bytes 25165824 | tf_op jit(solution)/shard_map/psum | solution.py:210
  860.8 9.8 copy-start.27
  860.8 9.8 copy-start.38
  860.8 9.8 copy-start.70
  883.6 348.2 %all-reduce.18.cloned.1.call-start = ((), (), s32[]{:S(2)}) async-start(), calls=%async_computation.9 | async-start | bytes 262144 | tf_op jit(solution)/shard_map/psum | solution.py:344
  898.7 111.6 %copy-start.52 = (bf16[128,768]{1,0:T(8,128)(2,1)S(1)}, bf16[128,768]{1,0:T(8,128)(2,1)}, u32[]{:S(2)}) copy-start(bf16[128,768]{1,0:T(8,128)(2,1)} %get-tuple-element.367) | copy-start | bytes 589828
  898.7 112.4 %copy-start.44 = (bf16[768,128]{0,1:T(8,128)(2,1)S(1)}, bf16[768,128]{0,1:T(8,128)(2,1)}, u32[]{:S(2)}) copy-start(bf16[768,128]{0,1:T(8,128)(2,1)} %copy-done.43) | copy-start | bytes 589828
  1021.7 424.2 %all-reduce.20.cloned.1.call-start = ((), (), s32[]{:S(2)}) async-start(), calls=%async_computation.10 | async-start | bytes 20054016 | tf_op jit(solution)/shard_map/psum | solution.py:344
  1029.9 144.6 %copy-start.57 = (bf16[8,2048,16]{1,2,0:T(8,128)(2,1)S(1)}, bf16[8,2048,16]{1,2,0:T(8,128)(2,1)}, u32[]{:S(2)}) copy-start(bf16[8,2048,16]{1,2,0:T(8,128)(2,1)} %param.46) | copy-start | bytes 1572868
  1029.9 144.6 %copy-start.90 = (f32[2048]{0:T(1024)S(1)}, f32[2048]{0:T(1024)}, u32[]{:S(2)}) copy-start(f32[2048]{0:T(1024)} %param.33) | copy-start | bytes 24580
  1174.5 8.8 slice-start.2
  1174.5 9.8 slice-start.10
  1174.5 10.4 slice-start.3
  1174.5 11.0 slice-start.11
  1174.5 11.0 copy-start.65
  1231.8 220.6 %copy-start.85 = (f32[8,16,64]{2,1,0:T(8,128)S(1)}, f32[8,16,64]{2,1,0:T(8,128)}, u32[]{:S(2)}) copy-start(f32[8,16,64]{2,1,0:T(8,128)} %get-tuple-element.657) | copy-start | bytes 98308
  1231.8 222.2 %copy-start.84 = (f32[8,16,64]{2,1,0:T(8,128)S(1)}, f32[8,16,64]{2,1,0:T(8,128)}, u32[]{:S(2)}) copy-start(f32[8,16,64]{2,1,0:T(8,128)} %get-tuple-element.659) | copy-start | bytes 98308
  1445.9 8.7 copy-start.73
  1445.9 9.4 copy-start.35
  1445.9 10.4 copy-start.34
  (73 other events, 305.2 us)
Sparse Core Ops, SparseCore 0:
  9.6 54.6 all-gather.5
  65.9 45.0 all-gather.7
  112.5 105.4 all-gather.13
  221.7 136.7 all-reduce.13
  359.9 106.6 all-gather.9
  468.1 104.9 all-gather.11
  602.2 161.8 all-reduce.15
  860.8 8.2 reduce-scatter.1
  883.7 290.6 all-reduce.21
  1177.3 54.4 all-reduce.17
  1236.4 209.4 all-reduce.19
where the time goes:
time: 1480 us; the launch traced here: 1470 us
  waiting for transfers between devices  874 us (59%)
  matrix products  271 us (18%)
  blocking collectives  229 us (15%)
  local copies, waits for them, and re-layouts  52.7 us (4%)
  other arithmetic  25.4 us (2%)
  between operations  15.4 us (1%)
    psum x2, waiting for transfers between devices, shards(): lax.psum((unflat_first(grad_query_first, query_first), unflat_second(grad...  252 us
    dot_general x45, matrix products, times_transposed(): lax.dot_general(left, right, (((1,), (1,)), ((), ())), preferred_element_...  141 us
    psum x1, waiting for transfers between devices, shards(): lax.psum((times(hidden, down_full), down_part), 'tp')  141 us
    psum x1, waiting for transfers between devices, shards(): lax.psum((times(att_low, output_full), out_part), 'tp')  131 us
    psum x1, blocking collectives, shards(): lax.psum((times(hidden, down_full), down_part), 'tp')  110 us
    all_gather x1, waiting for transfers between devices, shards(): lax.all_gather(frozen_local[4], 'fsdp', axis=0, tiled=True)  97.6 us
    all_gather x1, waiting for transfers between devices, shards(): lax.all_gather(frozen_local[5], 'fsdp', axis=0, tiled=True)  95.2 us
    psum x1, waiting for transfers between devices, shards(): lax.psum((times_transposed(grad_gate, gate_full) + times_transposed(grad_...  93.9 us
  transfers between devices with their start and end apart: 11, of which 9 were waited for; matrix products, arithmetic and copies ran while one was open for 13% of the time, Pallas kernels for 0%

commit v1 on v0

v1 whole, which is shorter than its diff:
```python
import functools

import jax
import jax.numpy as jnp
from jax import lax
from jax.experimental import pallas as pl
from jax.experimental.pallas import tpu as pltpu
from jax.sharding import PartitionSpec as P

HD = 64
RANK = 16
ADAPTERS = 8
PROMPT = 1024
CONT_LEN = 128
GROUP = 1536
BLOCK = 256


EPS = 1e-05
SCALE = 0.125
THETA = 10000.0
F32 = jnp.float32
BF16 = jnp.bfloat16


def dot(left, right, left_dim, right_dim):
    return lax.dot_general(
        left, right, (((left_dim,), (right_dim,)), ((), ())), preferred_element_type=F32
    )


def nn(left, right):
    return dot(left, right, 1, 0)


def nt(left, right):
    return dot(left, right, 1, 1)


def tn(left, right):
    return dot(left, right, 0, 0)


def layout(stream):
    in_prompt = stream < PROMPT
    later = jnp.maximum(stream - PROMPT, 0)
    sequence = jnp.where(in_prompt, 0, 1 + later // CONT_LEN)
    position = jnp.where(in_prompt, stream, PROMPT + later % CONT_LEN)
    return (sequence, position)


def selector(sequence, row_ids):
    places = jnp.arange(row_ids.shape[0], dtype=jnp.int32)
    chosen = jnp.sum(jnp.where(sequence[:, None] == places[None, :], row_ids[None, :], 0), axis=1)
    columns = jnp.arange(ADAPTERS * RANK, dtype=jnp.int32) // RANK
    return (chosen[:, None] == columns[None, :]).astype(F32)


def angles(position):
    freqs = THETA ** (-(jnp.arange(HD // 2, dtype=jnp.int32) * 2).astype(F32) / HD)
    turned = freqs[:, None] * position.astype(F32)[None, :]
    return (jnp.cos(turned), jnp.sin(turned))


def rotate(values, cosine, sine):
    half = HD // 2
    heads = values.shape[0] // HD
    split = values.reshape(heads, 2, half, values.shape[1])
    first = split[:, 0]
    second = split[:, 1]
    turned = jnp.stack(
        [first * cosine - second * sine, second * cosine + first * sine], axis=1
    )
    return turned.reshape(values.shape)


def first_rows(first):
    return jnp.transpose(first, (0, 2, 1)).reshape(first.shape[0] * first.shape[2], first.shape[1])


def second_rows(second):
    return second.reshape(second.shape[0] * second.shape[1], second.shape[2])


def unfirst(grad):
    return jnp.transpose(grad.reshape(ADAPTERS, RANK, grad.shape[1]), (0, 2, 1))


def unsecond(grad):
    return grad.reshape(ADAPTERS, RANK, grad.shape[1])


def rms_back(values, scaling, gain, grad_normed):
    weighted = grad_normed * gain
    return scaling * weighted - values * scaling * scaling * scaling * jnp.mean(
        weighted * values, axis=1, keepdims=True
    )


def diagonal_mask(block):
    key_at = lax.broadcasted_iota(jnp.int32, (BLOCK, BLOCK), 0)
    query_at = lax.broadcasted_iota(jnp.int32, (BLOCK, BLOCK), 1)
    same = (key_at // CONT_LEN) == (query_at // CONT_LEN)
    return (key_at <= query_at) & ((block < PROMPT // BLOCK) | same)


def forward_kernel(first_ref, k_ref, vt_ref, qt_ref, o_ref, lse_ref):
    block = first_ref[0] + pl.program_id(0)
    query = qt_ref[0]
    at = pl.multiple_of(block * BLOCK, BLOCK)
    masked = jnp.where(
        diagonal_mask(block), nn(k_ref[pl.ds(at, BLOCK), :], query) * SCALE, -1e30
    )
    value_own = vt_ref[:, pl.ds(at, BLOCK)]

    def finish(count):
        largest = jnp.max(masked, axis=0, keepdims=True)
        if count:
            scores = nn(k_ref[: count * BLOCK, :], query) * SCALE
            largest = jnp.maximum(largest, jnp.max(scores, axis=0, keepdims=True))
        expo = jnp.exp(masked - largest)
        total = jnp.sum(expo, axis=0, keepdims=True)
        out = nn(value_own, expo.astype(BF16))
        if count:
            expo = jnp.exp(scores - largest)
            total = total + jnp.sum(expo, axis=0, keepdims=True)
            out = out + nn(vt_ref[:, : count * BLOCK], expo.astype(BF16))
        o_ref[0] = (out / total).astype(BF16)
        lse_ref[0] = largest + jnp.log(total)

    seen = jnp.minimum(block, PROMPT // BLOCK)
    for count in range(PROMPT // BLOCK + 1):
        pl.when(seen == count)(functools.partial(finish, count))


def attend(first, key, value_t, query_t):
    heads, _, rows = query_t.shape
    whole = key.shape[0]
    spec = pl.BlockSpec((1, HD, BLOCK), lambda i, h, f: (h, 0, i))
    return pl.pallas_call(
        forward_kernel,
        out_shape=(
            jax.ShapeDtypeStruct((heads, HD, rows), BF16),
            jax.ShapeDtypeStruct((heads, 1, rows), F32),
        ),
        grid_spec=pltpu.PrefetchScalarGridSpec(
            num_scalar_prefetch=1,
            grid=(rows // BLOCK, heads),
            in_specs=[
                pl.BlockSpec((whole, HD), lambda i, h, f: (0, 0)),
                pl.BlockSpec((HD, whole), lambda i, h, f: (0, 0)),
                spec,
            ],
            out_specs=(spec, pl.BlockSpec((1, 1, BLOCK), lambda i, h, f: (h, 0, i))),
        ),
        cost_estimate=pl.CostEstimate(
            flops=heads * rows * whole * HD * 4,
            bytes_accessed=heads * rows * HD * 4,
            transcendentals=heads * rows * whole,
        ),
    )(first, key, value_t, query_t)


def backward_kernel(
    first_ref, k_ref, v_ref, kt_ref, qt_ref, ot_ref, dot_ref, lse_ref, dq_ref, dkv_ref
):
    block = first_ref[0] + pl.program_id(0)

    @pl.when((pl.program_id(0) == 0) & (pl.program_id(1) == 0))
    def _():
        dkv_ref[...] = jnp.zeros_like(dkv_ref)

    query = qt_ref[0]
    grad = dot_ref[0]
    logs = lse_ref[0]
    delta = jnp.sum(grad.astype(F32) * ot_ref[0].astype(F32), axis=0, keepdims=True)
    at = pl.multiple_of(block * BLOCK, BLOCK)

    def part(key_rows, value_rows, allowed):
        scores = nn(key_rows, query) * SCALE
        if allowed is not None:
            scores = jnp.where(allowed, scores, -1e30)
        probs = jnp.exp(scores - logs)
        grad_probs = nn(value_rows, grad)
        grad_scores = (probs * (grad_probs - delta)).astype(BF16)
        return (
            grad_scores,
            nt(query, grad_scores) * SCALE,
            nt(grad, probs.astype(BF16)),
        )

    def finish(count):
        own = pl.ds(at, BLOCK)
        grad_scores, grad_key, grad_value = part(
            k_ref[own, :], v_ref[own, :], diagonal_mask(block)
        )
        dkv_ref[:HD, own] += grad_key
        dkv_ref[HD:, own] += grad_value
        grad_query = nn(kt_ref[:, own], grad_scores)
        if count:
            grad_scores, grad_key, grad_value = part(
                k_ref[: count * BLOCK, :], v_ref[: count * BLOCK, :], None
            )
            dkv_ref[:HD, : count * BLOCK] += grad_key
            dkv_ref[HD:, : count * BLOCK] += grad_value
            grad_query = grad_query + nn(kt_ref[:, : count * BLOCK], grad_scores)
        dq_ref[0] = grad_query * SCALE

    seen = jnp.minimum(block, PROMPT // BLOCK)
    for count in range(PROMPT // BLOCK + 1):
        pl.when(seen == count)(functools.partial(finish, count))


def attend_back(first, key, value, key_t, query_t, out_t, grad_t, logs):
    heads, _, rows = query_t.shape
    whole = key.shape[0]
    spec = pl.BlockSpec((1, HD, BLOCK), lambda i, h, f: (h, 0, i))
    row = pl.BlockSpec((whole, HD), lambda i, h, f: (0, 0))
    return pl.pallas_call(
        backward_kernel,
        out_shape=(
            jax.ShapeDtypeStruct((heads, HD, rows), F32),
            jax.ShapeDtypeStruct((2 * HD, whole), F32),
        ),
        grid_spec=pltpu.PrefetchScalarGridSpec(
            num_scalar_prefetch=1,
            grid=(rows // BLOCK, heads),
            in_specs=[
                row,
                row,
                pl.BlockSpec((HD, whole), lambda i, h, f: (0, 0)),
                spec,
                spec,
                spec,
                pl.BlockSpec((1, 1, BLOCK), lambda i, h, f: (h, 0, i)),
            ],
            out_specs=(spec, pl.BlockSpec((2 * HD, whole), lambda i, h, f: (0, 0))),
        ),
        cost_estimate=pl.CostEstimate(
            flops=heads * rows * whole * HD * 10,
            bytes_accessed=heads * rows * HD * 10,
            transcendentals=heads * rows * whole,
        ),
    )(first, key, value, key_t, query_t, out_t, grad_t, logs)


def flipped(bit):
    return [(place, place ^ bit) for place in range(4)]


def bit_of(bit):
    return (lax.axis_index("tp") // bit) % 2


def reduce_rows(partial, bit):
    other = 3 - bit
    half = partial.shape[0] // 2
    quarter = half // 2
    mine = bit_of(bit)
    then = bit_of(other)
    sent = lax.dynamic_slice_in_dim(partial, (1 - mine) * half, half, 0)
    kept = lax.dynamic_slice_in_dim(partial, mine * half, half, 0)
    came = lax.ppermute(sent, "tp", flipped(bit))
    summed = kept.astype(F32) + came.astype(F32)
    sent = lax.dynamic_slice_in_dim(summed, (1 - then) * quarter, quarter, 0).astype(BF16)
    kept = lax.dynamic_slice_in_dim(summed, then * quarter, quarter, 0)
    came = lax.ppermute(sent, "tp", flipped(other))
    return kept + came.astype(F32)


def gather_rows(own, bit):
    other = 3 - bit
    mine = bit_of(bit)
    then = bit_of(other)
    came = lax.ppermute(own, "tp", flipped(other))
    pair = jnp.where(
        then == 0, jnp.concatenate([own, came], axis=0), jnp.concatenate([came, own], axis=0)
    )
    came = lax.ppermute(pair, "tp", flipped(bit))
    return jnp.where(
        mine == 0, jnp.concatenate([pair, came], axis=0), jnp.concatenate([came, pair], axis=0)
    )


def shards(
    tokens,
    cotangent,
    adapter_ids,
    gain_attn,
    gain_mlp,
    query_weight,
    key_weight,
    value_weight,
    output_weight,
    gate_weight,
    up_weight,
    down_weight,
    query_first,
    query_second,
    key_first,
    key_second,
    value_first,
    value_second,
    output_first,
    output_second,
    gate_first,
    gate_second,
    up_first,
    up_second,
    down_first,
    down_second,
):
    rows, width = tokens.shape
    q_width = query_weight.shape[1]
    heads = q_width // HD
    inner = ADAPTERS * RANK
    core = lax.axis_index("ctx")
    place = lax.axis_index("tp")
    stream = core * rows + jnp.arange(rows, dtype=jnp.int32)
    sequence, position = layout(stream)
    row_ids = lax.dynamic_index_in_dim(adapter_ids, lax.axis_index("fsdp"), 0, False)
    select = selector(sequence, row_ids)
    select_low = select.astype(BF16)
    cosine, sine = angles(position)
    first_block = (core * (rows // BLOCK)).astype(jnp.int32).reshape(1)
    chunk = rows // 2
    bits = (1, 2)
    starts = [
        index * chunk + bit_of(bit) * (chunk // 2) + bit_of(3 - bit) * (chunk // 4)
        for index, bit in enumerate(bits)
    ]

    def own_rows(array, index):
        return lax.dynamic_slice_in_dim(array, starts[index], chunk // 4, 0)

    def chunk_of(array, index):
        return lax.slice_in_dim(array, index * chunk, (index + 1) * chunk, axis=0)

    def gathered(local):
        half = local.shape[0] // 2
        part = lax.dynamic_slice_in_dim(local, core * half, half, 0)
        return lax.all_gather(part, ("fsdp", "ctx"), axis=0, tiled=True)

    qkv_full = gathered(jnp.concatenate([query_weight, key_weight, value_weight], axis=1))
    output_full = gathered(output_weight.T)
    gate_full = gathered(gate_weight)
    up_full = gathered(up_weight)
    down_full = gathered(down_weight.T)

    firsts = jnp.concatenate(
        [first_rows(query_first), first_rows(key_first), first_rows(value_first)], axis=0
    )
    query_rows = second_rows(query_second)
    key_rows = second_rows(key_second)
    value_rows = second_rows(value_second)
    output_rows = second_rows(output_second)
    gate_rows = second_rows(gate_second)
    up_rows = second_rows(up_second)
    down_rows = second_rows(down_second)
    output_cols = first_rows(output_first)
    gate_cols = first_rows(gate_first)
    up_cols = first_rows(up_first)
    down_cols = first_rows(down_first)

    source = tokens.astype(F32)
    scale_one = lax.rsqrt(jnp.mean(source * source, axis=1, keepdims=True) + EPS)
    normed = (source * scale_one * gain_attn).astype(BF16)
    triple = jnp.concatenate([select, select, select], axis=1)
    qkv_inner = (nt(normed, firsts) * triple).astype(BF16)
    query_inner = qkv_inner[:, :inner]
    key_inner = qkv_inner[:, inner : 2 * inner]
    value_inner = qkv_inner[:, 2 * inner :]
    projected = dot(qkv_full, normed, 0, 1)
    query_t = projected[:q_width] + dot(query_rows, query_inner, 0, 1)
    key_t = projected[q_width : q_width + HD] + dot(key_rows, key_inner, 0, 1)
    value_t = projected[q_width + HD :] + dot(value_rows, value_inner, 0, 1)
    query_rot = rotate(query_t, cosine, sine).astype(BF16).reshape(heads, HD, rows)
    kv_local = jnp.concatenate([rotate(key_t, cosine, sine), value_t], axis=0).astype(BF16)
    kv_other = lax.ppermute(kv_local, "ctx", [(0, 1), (1, 0)])
    kv_t = jnp.where(
        core == 0,
        jnp.concatenate([kv_local, kv_other], axis=1),
        jnp.concatenate([kv_other, kv_local], axis=1),
    )
    key_whole = kv_t[:HD].T
    value_whole = kv_t[HD:].T
    attended_t, log_total = attend(first_block, key_whole, kv_t[HD:], query_rot)
    att_t = attended_t.reshape(q_width, rows)

    middle, scale_two, spread = [], [], []
    out_weights = jnp.concatenate([output_full, output_cols], axis=0)
    for index, bit in enumerate(bits):
        cols = lax.slice_in_dim(att_t, index * chunk, (index + 1) * chunk, axis=1)
        total = reduce_rows(dot(cols, out_weights, 0, 1).astype(BF16), bit)
        out_inner = (total[:, width:] * own_rows(select, index)).astype(BF16)
        mid = own_rows(tokens, index).astype(F32) + total[:, :width] + nn(out_inner, output_rows)
        scaling = lax.rsqrt(jnp.mean(mid * mid, axis=1, keepdims=True) + EPS)
        normed_own = (mid * scaling * gain_mlp).astype(BF16)
        middle.append(mid)
        scale_two.append(scaling)
        spread.append(gather_rows(jnp.concatenate([normed_own, out_inner], axis=1), bit))

    grad_down_inner = nt(cotangent, down_rows).astype(BF16) * select_low
    hidden_all, grad_gate_all, grad_upper_all, gate_inner_all, up_inner_all = [], [], [], [], []
    back_parts, down_parts = [], []
    inner_cols = jnp.concatenate([gate_cols, up_cols], axis=0)
    for index, bit in enumerate(bits):
        normed_two = spread[index][:, :width]
        sel = chunk_of(select, index)
        both = nt(normed_two, inner_cols)
        gate_inner = (both[:, :inner] * sel).astype(BF16)
        up_inner = (both[:, inner:] * sel).astype(BF16)
        gate = nn(normed_two, gate_full) + nn(gate_inner, gate_rows)
        upper = nn(normed_two, up_full) + nn(up_inner, up_rows)
        sigmoid = jax.nn.sigmoid(gate)
        swish = gate * sigmoid
        hidden = (swish * upper).astype(BF16)
        grad_hidden = nn(chunk_of(cotangent, index), down_full) + nn(
            chunk_of(grad_down_inner, index), down_cols
        )
        grad_gate = (grad_hidden * upper * (sigmoid * (1.0 + gate * (1.0 - sigmoid)))).astype(BF16)
        grad_upper = (grad_hidden * swish).astype(BF16)
        back_parts.append(
            jnp.concatenate(
                [
                    (nt(grad_gate, gate_full) + nt(grad_upper, up_full)).astype(BF16),
                    nt(grad_gate, gate_rows).astype(BF16),
                    nt(grad_upper, up_rows).astype(BF16),
                ],
                axis=1,
            )
        )
        down_parts.append(
            jnp.concatenate(
                [nt(hidden, down_full).astype(BF16), nt(hidden, down_cols).astype(BF16)], axis=1
            )
        )
        hidden_all.append(hidden)
        grad_gate_all.append(grad_gate)
        grad_upper_all.append(grad_upper)
        gate_inner_all.append(gate_inner)
        up_inner_all.append(up_inner)

    grad_middle, grad_spread = [], []
    for index, bit in enumerate(bits):
        total = reduce_rows(back_parts[index], bit)
        sel = own_rows(select_low, index)
        grad_gate_inner = total[:, width : width + inner].astype(BF16) * sel
        grad_up_inner = total[:, width + inner :].astype(BF16) * sel
        grad_normed = total[:, :width] + nn(grad_gate_inner, gate_cols) + nn(grad_up_inner, up_cols)
        grad_mid = own_rows(cotangent, index).astype(F32) + rms_back(
            middle[index], scale_two[index], gain_mlp, grad_normed
        )
        grad_middle.append(grad_mid)
        grad_spread.append(
            gather_rows(
                jnp.concatenate([grad_mid.astype(BF16), grad_gate_inner, grad_up_inner], axis=1),
                bit,
            )
        )

    grad_att_t, grad_out_inner = [], []
    for index in range(2):
        branch = grad_spread[index][:, :width]
        grad_inner = nt(branch, output_rows).astype(BF16) * chunk_of(select_low, index)
        grad_out_inner.append(grad_inner)
        grad_att_t.append(
            (dot(output_full, branch, 0, 1) + dot(output_cols, grad_inner, 0, 1)).astype(BF16)
        )
    grad_heads = jnp.concatenate(grad_att_t, axis=1).reshape(heads, HD, rows)
    grad_query_rot, kv_grad = attend_back(
        first_block,
        key_whole,
        value_whole,
        kv_t[:HD],
        query_rot,
        attended_t,
        grad_heads,
        log_total,
    )
    sent = lax.dynamic_slice_in_dim(kv_grad, (1 - core) * rows, rows, 1)
    kept = lax.dynamic_slice_in_dim(kv_grad, core * rows, rows, 1)
    kv_sum = kept + lax.ppermute(sent, "ctx", [(0, 1), (1, 0)])
    grad_query_t = rotate(grad_query_rot.reshape(q_width, rows), cosine, -sine).astype(BF16)
    grad_key_t = rotate(kv_sum[:HD], cosine, -sine).astype(BF16)
    grad_value_t = kv_sum[HD:].astype(BF16)
    grad_qkv_t = jnp.concatenate([grad_query_t, grad_key_t, grad_value_t], axis=0)

    input_parts, qkv_spread = [], []
    for index, bit in enumerate(bits):
        cols = lax.slice_in_dim(grad_qkv_t, index * chunk, (index + 1) * chunk, axis=1)
        part = jnp.concatenate(
            [
                dot(cols, qkv_full, 0, 1).astype(BF16),
                dot(cols[:q_width], query_rows, 0, 1).astype(BF16),
                dot(cols[q_width : q_width + HD], key_rows, 0, 1).astype(BF16),
                dot(cols[q_width + HD :], value_rows, 0, 1).astype(BF16),
            ],
            axis=1,
        )
        total = reduce_rows(part, bit)
        sel = own_rows(select_low, index)
        inners = total[:, width:].astype(BF16) * jnp.concatenate([sel, sel, sel], axis=1)
        grad_normed = total[:, :width] + nn(inners, firsts)
        own = grad_middle[index] + rms_back(
            own_rows(tokens, index).astype(F32),
            own_rows(scale_one, index),
            gain_attn,
            grad_normed,
        )
        whole = gather_rows(jnp.concatenate([own.astype(BF16), inners], axis=1), bit)
        input_parts.append(whole[:, :width].astype(F32))
        qkv_spread.append(whole[:, width:])
    input_grad = jnp.concatenate(input_parts, axis=0)

    output_parts, down_inner_all = [], []
    for index, bit in enumerate(bits):
        total = reduce_rows(down_parts[index], bit)
        down_inner = (total[:, width:] * own_rows(select, index)).astype(BF16)
        own = middle[index] + total[:, :width] + nn(down_inner, down_rows)
        whole = gather_rows(jnp.concatenate([own.astype(BF16), down_inner], axis=1), bit)
        output_parts.append(whole[:, :width])
        down_inner_all.append(whole[:, width:])
    output = jnp.concatenate(output_parts, axis=0)

    quarter = inner // 4

    def share(array):
        return lax.dynamic_slice_in_dim(array, place * quarter, quarter, 1)

    join = functools.partial(jnp.concatenate, axis=0)
    spread_two = join(spread)
    normed_two = spread_two[:, :width]
    out_inner = spread_two[:, width:]
    back_two = join(grad_spread)
    branch = back_two[:, :width]
    inner_two = back_two[:, width:]
    down_inner = join(down_inner_all)
    hidden = join(hidden_all)
    grad_gate = join(grad_gate_all)
    grad_upper = join(grad_upper_all)
    early = (
        tn(share(inner_two[:, :inner]), normed_two),
        tn(share(inner_two[:, inner:]), normed_two),
        tn(share(out_inner), branch),
        tn(share(down_inner), cotangent),
        tn(grad_down_inner, hidden),
        tn(join(gate_inner_all), grad_gate),
        tn(join(up_inner_all), grad_upper),
        dot(join(grad_out_inner), att_t, 0, 1),
    )
    early = lax.psum(tuple(a.astype(BF16) for a in early), ("fsdp", "ctx"))
    shared = lax.all_gather(jnp.concatenate(early[:4], axis=1), "tp", axis=0, tiled=True)
    gate_first_grad, up_first_grad, output_second_grad, down_second_grad = (
        lax.slice_in_dim(shared, i * width, (i + 1) * width, axis=1).astype(F32) for i in range(4)
    )
    down_first_grad, gate_second_grad, up_second_grad, output_first_grad = (
        a.astype(F32) for a in early[4:]
    )
    inners = join(qkv_spread)
    late = (
        tn(share(inners[:, :inner]), normed),
        tn(share(inners[:, inner : 2 * inner]), normed),
        tn(share(inners[:, 2 * inner :]), normed),
        dot(query_inner, grad_query_t, 0, 1),
        dot(jnp.concatenate([key_inner, value_inner], axis=1), grad_qkv_t[q_width:], 0, 1),
    )
    late = lax.psum(tuple(a.astype(BF16) for a in late), ("fsdp", "ctx"))
    shared = lax.all_gather(jnp.concatenate(late[:3], axis=1), "tp", axis=0, tiled=True)
    query_first_grad, key_first_grad, value_first_grad = (
        lax.slice_in_dim(shared, i * width, (i + 1) * width, axis=1).astype(F32) for i in range(3)
    )
    query_second_grad = late[3].astype(F32)
    key_second_grad = late[4][:inner, :HD].astype(F32)
    value_second_grad = late[4][inner:, HD:].astype(F32)
    return (
        output,
        input_grad,
        unfirst(query_first_grad),
        unsecond(query_second_grad),
        unfirst(key_first_grad),
        unsecond(key_second_grad),
        unfirst(value_first_grad),
        unsecond(value_second_grad),
        unfirst(output_first_grad),
        unsecond(output_second_grad),
        unfirst(gate_first_grad),
        unsecond(gate_second_grad),
        unfirst(up_first_grad),
        unsecond(up_second_grad),
        unfirst(down_first_grad),
        unsecond(down_second_grad),
    )


def solution(mesh):
    placed = (
        P(("fsdp", "ctx"), None),
        P(("fsdp", "ctx"), None),
        P(),
        P(),
        P(),
        P("fsdp", "tp"),
        P("fsdp", "tp"),
        P("fsdp", "tp"),
        P("tp", "fsdp"),
        P("fsdp", "tp"),
        P("fsdp", "tp"),
        P("tp", "fsdp"),
        P(),
        P(None, None, "tp"),
        P(),
        P(None, None, "tp"),
        P(),
        P(None, None, "tp"),
        P(None, "tp", None),
        P(),
        P(),
        P(None, None, "tp"),
        P(),
        P(None, None, "tp"),
        P(None, "tp", None),
        P(),
    )
    return jax.shard_map(
        shards,
        mesh=mesh,
        in_specs=placed,
        out_specs=(
            P(("fsdp", "ctx"), None),
            P(("fsdp", "ctx"), None),
            P(),
            P(None, None, "tp"),
            P(),
            P(None, None, "tp"),
            P(),
            P(None, None, "tp"),
            P(None, "tp", None),
            P(),
            P(),
            P(None, None, "tp"),
            P(),
            P(None, None, "tp"),
            P(None, "tp", None),
            P(),
        ),
        check_vma=False,
    )
```

time: 1480 us -> 728 us (0.49)
  waiting for transfers between devices: 874 us -> 409 us
  blocking collectives: 229 us -> 0 us
  matrix products: 271 us -> 118 us
  starting transfers between devices: 0.44 us -> 46.5 us
  Pallas kernels: 0 us -> 39 us
  other arithmetic: 25.4 us -> 51.5 us
  local copies, waits for them, and re-layouts: 52.7 us -> 35.9 us
    psum x5 -> x1, waiting for transfers between devices: 618 us -> 69.2 us  [shards(): late = lax.psum(tuple((a.astype(BF16) for a in late)), ('fsdp', 'ctx'))]
    psum x3 -> x0, blocking collectives: 193 us -> none  [the longest x1 110 us: shards(): lax.psum((times(hidden, down_full), down_part), 'tp')]
    ppermute x0 -> x34, waiting for transfers between devices: none -> 187 us  [the longest x8 64 us: reduce_rows(): came = lax.ppermute(sent, 'tp', flipped(bit))]
    dot_general x112 -> x71, matrix products: 271 us -> 118 us  [dot(): lax.dot_general(left, right, (((left_dim,), (right_dim,)), ((), ())), pre...]
    all_gather x5 -> x7, waiting for transfers between devices: 253 us -> 153 us  [the longest x5 105 us: gathered(): return lax.all_gather(part, ('fsdp', 'ctx'), axis=0, tiled=True)]
    ppermute x0 -> x34, starting transfers between devices: none -> 46 us  [the longest x8 11 us: gather_rows(): came = lax.ppermute(pair, 'tp', flipped(bit))]
    pallas_call x0 -> x2, Pallas kernels: none -> 39 us  [the longest x1 20.8 us: attend_back(): pl.pallas_call(backward_kernel, out_shape=(jax.ShapeDtypeStruct((heads, H...]
    all_gather x3 -> x0, blocking collectives: 35.9 us -> none  [the longest x1 16.8 us: shards(): lax.all_gather(frozen_local[2], 'fsdp', axis=0, tiled=True)]
  transfers between devices with their start and end apart: 11 -> 42, of which waited for: 9 -> 34; matrix products, arithmetic and copies ran while one was open for 13% -> 19% of each run, Pallas kernels for 0% -> 3%
where the time goes in v1:
time: 728 us; the launch traced here: 717 us
  waiting for transfers between devices  409 us (56%)
  matrix products  118 us (16%)
  other arithmetic  51.5 us (7%)
  starting transfers between devices  46.5 us (6%)
  Pallas kernels  39 us (5%)
  local copies, waits for them, and re-layouts  35.9 us (5%)
  between operations  16.8 us (2%)
    dot_general x71, matrix products, dot(): lax.dot_general(left, right, (((left_dim,), (right_dim,)), ((), ())), pre...  118 us
    all_gather x5, waiting for transfers between devices, gathered(): return lax.all_gather(part, ('fsdp', 'ctx'), axis=0, tiled=True)  105 us
    psum x1, waiting for transfers between devices, shards(): late = lax.psum(tuple((a.astype(BF16) for a in late)), ('fsdp', 'ctx'))  69.2 us
    ppermute x8, waiting for transfers between devices, reduce_rows(): came = lax.ppermute(sent, 'tp', flipped(bit))  64 us
    ppermute x8, waiting for transfers between devices, gather_rows(): came = lax.ppermute(pair, 'tp', flipped(bit))  57.8 us
    ppermute x8, waiting for transfers between devices, gather_rows(): came = lax.ppermute(own, 'tp', flipped(other))  33.9 us
    all_gather x1, waiting for transfers between devices, shards(): lax.all_gather(jnp.concatenate(early[:4], axis=1), 'tp', axis=0, tiled=True)  33 us
    ppermute x8, waiting for transfers between devices, reduce_rows(): came = lax.ppermute(sent, 'tp', flipped(other))  31.3 us
  transfers between devices with their start and end apart: 42, of which 34 were waited for; matrix products, arithmetic and copies ran while one was open for 19% of the time, Pallas kernels for 3%

profile of v1, /device:TPU:0, one launch (start us, length us, event | category | flops | bytes accessed | tf_op | source)
XLA Modules:
  0.0 717.0 jit_solution(18311909141606087115)
XLA Ops:
  21.2 2.6 fusion.28
  23.8 24.1 %all-gather.8.cloned.1.call-done = bf16[2048,640]{1,0:T(8,128)(2,1)} async-done(((bf16[256,640]{1,0:T(8,128)(2,1)}), bf16[2048,640]{1,0:T(8,128)(2,1)}) %all-gather.8.cloned.1.call-update) | async-done | bytes 2621456 | tf_op jit(solution)/shard_map/all_gather | solution.py:342
  47.9 4.0 fusion.220
  56.9 18.2 %shard_map.369 = (bf16[8,64,768]{2,1,0:T(8,128)(2,1)}, f32[8,1,768]{2,1,0:T(1,128)}) custom-call(s32[1]{0:T(128)} %bitcast.first_ref, bf16[1536,64]{1,0:T(8,128)(2,1)} %copy.63.k_ref, bf16[64,1536]{1,0:T(8,128)(2,1)} %get-tuple-element.88.vt_ref, bf16[8,64,768]{2,1,0:T(8,128)(2,1)} %bitcast.245), custom_call_target="tpu_custom_call" | custom-call | flops 2415919104 | bytes 1572864 | tf_op jit(solution)/shard_map/pallas_call | solution.py:140
  75.1 4.8 all-gather.10.cloned.1.call-done
  79.9 2.8 convolution_convert_fusion
  86.2 2.9 convolution_convert_fusion.1
  90.6 13.0 %collective-permute-done.9 = bf16[192,2176]{1,0:T(8,128)(2,1)S(1)} collective-permute-done((bf16[192,2176]{1,0:T(8,128)(2,1)}, bf16[192,2176]{1,0:T(8,128)(2,1)S(1)}, u32[]{:S(2)}, u32[]{:S(2)}) %collective-permute-start.9) | collective-permute-done | bytes 835616 | tf_op jit(solution)/shard_map/ppermute | solution.py:263
  104.8 3.9 collective-permute-done.1
  109.6 8.1 %collective-permute-done.10 = bf16[96,2176]{1,0:T(8,128)(2,1)S(1)} collective-permute-done((bf16[96,2176]{1,0:T(8,128)(2,1)S(1)}, bf16[96,2176]{1,0:T(8,128)(2,1)S(1)}, u32[]{:S(2)}, u32[]{:S(2)}) %collective-permute-start.10) | collective-permute-done | bytes 417824 | tf_op jit(solution)/shard_map/ppermute | solution.py:267
  123.2 7.9 %collective-permute-done.11 = bf16[96,2176]{1,0:T(8,128)(2,1)} collective-permute-done((bf16[96,2176]{1,0:T(8,128)(2,1)S(1)}, bf16[96,2176]{1,0:T(8,128)(2,1)}, u32[]{:S(2)}, u32[]{:S(2)}) %collective-permute-start.11) | collective-permute-done | bytes 417824 | tf_op jit(solution)/shard_map/ppermute | solution.py:275
  136.7 3.7 fusion.49
  142.0 10.3 %collective-permute-done.12 = bf16[192,2176]{1,0:T(8,128)(2,1)} collective-permute-done((bf16[192,2176]{1,0:T(8,128)(2,1)S(1)}, bf16[192,2176]{1,0:T(8,128)(2,1)}, u32[]{:S(2)}, u32[]{:S(2)}) %collective-permute-start.12) | collective-permute-done | bytes 835616 | tf_op jit(solution)/shard_map/ppermute | solution.py:279
  167.3 5.9 convolution_bitcast_fusion
  176.0 2.9 convolution_bitcast_fusion.1
  180.7 22.1 %all-gather.14.cloned.1.call-done = bf16[2048,1408]{1,0:T(8,128)(2,1)} async-done(((bf16[256,1408]{1,0:T(8,128)(2,1)}), bf16[2048,1408]{1,0:T(8,128)(2,1)}) %all-gather.14.cloned.1.call-update) | async-done | bytes 5767184 | tf_op jit(solution)/shard_map/all_gather | solution.py:342
  202.8 6.8 convolution_add_fusion.2
  209.6 54.4 %all-gather.12.cloned.1.call-done = bf16[2048,1408]{1,0:T(8,128)(2,1)} async-done(((bf16[256,1408]{1,0:T(8,128)(2,1)}), bf16[2048,1408]{1,0:T(8,128)(2,1)}) %all-gather.12.cloned.1.call-update) | async-done | bytes 5767184 | tf_op jit(solution)/shard_map/all_gather | solution.py:342
  264.0 7.7 %multiply_convert_fusion.1 = (bf16[384,1408]{1,0:T(8,128)(2,1)S(1)}, bf16[384,1408]{1,0:T(8,128)(2,1)S(1)}, bf16[384,1408]{1,0:T(8,128)(2,1)S(1)}) fusion(f32[384,1408]{1,0:T(8,128)} %convolution_add_fusion, f32[384,1408]{1,0:T(8,128)} %convolution_add_fusion.2, f32[384,1408]{1,0:T(8,128)} %fusion.224, ...), kind=kOutput, calls=%fused_computation.54 | convolution fusion | flops 2223243264 | bytes 17072128 | tf_op jit(solution)/shard_map/dot_general | solution.py:27
  272.7 4.3 fusion.228
  277.0 4.3 add_convert_fusion
  283.4 4.0 convolution_add_fusion.4
  287.5 5.1 multiply_convert_fusion.3
  293.5 5.2 fusion.226
  298.8 2.6 add_convert_fusion.1
  303.7 2.6 convolution_convert_fusion.4
  313.0 13.8 %collective-permute-done.13 = bf16[192,2176]{1,0:T(8,128)(2,1)S(1)} collective-permute-done((bf16[192,2176]{1,0:T(8,128)(2,1)S(1)}, bf16[192,2176]{1,0:T(8,128)(2,1)S(1)}, u32[]{:S(2)}, u32[]{:S(2)}) %collective-permute-start.13) | collective-permute-done | bytes 835616 | tf_op jit(solution)/shard_map/ppermute | solution.py:263
  328.1 14.0 %collective-permute-done.5 = bf16[192,2176]{1,0:T(8,128)(2,1)S(1)} collective-permute-done((bf16[192,2176]{1,0:T(8,128)(2,1)S(1)}, bf16[192,2176]{1,0:T(8,128)(2,1)S(1)}, u32[]{:S(2)}, u32[]{:S(2)}) %collective-permute-start.5) | collective-permute-done | bytes 835616 | tf_op jit(solution)/shard_map/ppermute | solution.py:263
  346.5 4.5 collective-permute-done.14
  351.1 3.9 collective-permute-done.6
  356.7 3.2 collective-permute-done.22
  370.1 8.9 %collective-permute-done.15 = bf16[96,2176]{1,0:T(8,128)(2,1)S(1)} collective-permute-done((bf16[96,2176]{1,0:T(8,128)(2,1)S(1)}, bf16[96,2176]{1,0:T(8,128)(2,1)S(1)}, u32[]{:S(2)}, u32[]{:S(2)}) %collective-permute-start.15) | collective-permute-done | bytes 417824 | tf_op jit(solution)/shard_map/ppermute | solution.py:275
  384.8 3.6 collective-permute-done.23
  390.3 10.4 %collective-permute-done.16 = bf16[192,2176]{1,0:T(8,128)(2,1)S(1)} collective-permute-done((bf16[192,2176]{1,0:T(8,128)(2,1)S(1)}, bf16[192,2176]{1,0:T(8,128)(2,1)S(1)}, u32[]{:S(2)}, u32[]{:S(2)}) %collective-permute-start.16) | collective-permute-done | bytes 835616 | tf_op jit(solution)/shard_map/ppermute | solution.py:279
  406.2 8.5 %collective-permute-done.24 = bf16[192,2304]{1,0:T(8,128)(2,1)S(1)} collective-permute-done((bf16[192,2304]{1,0:T(8,128)(2,1)S(1)}, bf16[192,2304]{1,0:T(8,128)(2,1)S(1)}, u32[]{:S(2)}, u32[]{:S(2)}) %collective-permute-start.24) | collective-permute-done | bytes 884768 | tf_op jit(solution)/shard_map/ppermute | solution.py:279
  422.8 20.8 %shard_map.370 = (f32[8,64,768]{2,1,0:T(8,128)}, f32[128,1536]{1,0:T(8,128)}) custom-call(s32[1]{0:T(128)} %bitcast.first_ref, bf16[1536,64]{1,0:T(8,128)(2,1)} %copy.63.k_ref, bf16[1536,64]{1,0:T(8,128)(2,1)} %copy.73.v_ref, bf16[64,1536]{1,0:T(8,128)(2,1)} %get-tuple-element.85.kt_ref, bf16[8,64,768]{2,1,0:T(8,128)(2,1)} %bitcast.246, ...), custom_call_target="tpu_custom_call" | custom-call | flops 6039797760 | bytes 3932160 | tf_op jit(solution)/shard_map/pallas_call | solution.py:219
  449.2 5.7 collective-permute-start.25
  466.0 19.1 %collective-permute-done.26 = bf16[192,2432]{1,0:T(8,128)(2,1)S(1)} collective-permute-done((bf16[192,2432]{1,0:T(8,128)(2,1)S(1)}, bf16[192,2432]{1,0:T(8,128)(2,1)S(1)}, u32[]{:S(2)}, u32[]{:S(2)}) %collective-permute-start.26) | collective-permute-done | bytes 933920 | tf_op jit(solution)/shard_map/ppermute | solution.py:263
  487.4 2.7 collective-permute-start.31
  490.1 7.1 collective-permute-done.27
  508.8 8.3 %collective-permute-done.7 = bf16[96,2176]{1,0:T(8,128)(2,1)S(1)} collective-permute-done((bf16[96,2176]{1,0:T(8,128)(2,1)S(1)}, bf16[96,2176]{1,0:T(8,128)(2,1)S(1)}, u32[]{:S(2)}, u32[]{:S(2)}) %collective-permute-start.7) | collective-permute-done | bytes 417824 | tf_op jit(solution)/shard_map/ppermute | solution.py:275
  519.7 4.0 collective-permute-done.28
  528.2 10.7 %collective-permute-done.8 = bf16[192,2176]{1,0:T(8,128)(2,1)S(1)} collective-permute-done((bf16[192,2176]{1,0:T(8,128)(2,1)S(1)}, bf16[192,2176]{1,0:T(8,128)(2,1)S(1)}, u32[]{:S(2)}, u32[]{:S(2)}) %collective-permute-start.8) | collective-permute-done | bytes 835616 | tf_op jit(solution)/shard_map/ppermute | solution.py:279
  540.9 14.9 %collective-permute-done.29 = bf16[192,2432]{1,0:T(8,128)(2,1)S(1)} collective-permute-done((bf16[192,2432]{1,0:T(8,128)(2,1)S(1)}, bf16[192,2432]{1,0:T(8,128)(2,1)S(1)}, u32[]{:S(2)}, u32[]{:S(2)}) %collective-permute-start.29) | collective-permute-done | bytes 933920 | tf_op jit(solution)/shard_map/ppermute | solution.py:279
  563.9 69.2 %all-reduce.3.cloned.1.call-done = (bf16[32,2048]{1,0:T(8,128)(2,1)}, bf16[32,2048]{1,0:T(8,128)(2,1)}, bf16[32,2048]{1,0:T(8,128)(2,1)}, bf16[8,16,512]{2,1,0:T...) async-done(((bf16[32,2048]{1,0:T(8,128)(2,1)}, ...) | async-done | bytes 2326544 | tf_op jit(solution)/shard_map/psum | solution.py:568
  642.4 3.5 maximum_convert_fusion
  651.5 14.4 %all-gather.18.cloned.1.call-done = bf16[128,6144]{1,0:T(8,128)(2,1)} async-done(((bf16[32,6144]{1,0:T(8,128)(2,1)}), bf16[128,6144]{1,0:T(8,128)(2,1)}) %all-gather.18.cloned.1.call-update) | async-done | bytes 1572880 | tf_op jit(solution)/shard_map/all_gather | solution.py:569
  670.7 33.0 %all-gather.20.cloned.1.call-done = bf16[128,8192]{1,0:T(8,128)(2,1)} async-done(((bf16[32,8192]{1,0:T(8,128)(2,1)}), bf16[128,8192]{1,0:T(8,128)(2,1)}) %all-gather.20.cloned.1.call-update) | async-done | bytes 2097168 | tf_op jit(solution)/shard_map/all_gather | solution.py:553
  (504 shorter events, 181.5 us)
Async XLA Ops:
  7.2 40.7 %all-gather.8.cloned.1.call-start = ((), (), s32[]{:S(2)}) async-start(), calls=%async_computation | async-start | bytes 2949120 | tf_op jit(solution)/shard_map/all_gather | solution.py:342
  11.1 68.8 %all-gather.10.cloned.1.call-start = ((), (), s32[]{:S(2)}) async-start(), calls=%async_computation.1 | async-start | bytes 2359296 | tf_op jit(solution)/shard_map/all_gather | solution.py:342
  12.0 155.4 %all-gather.16.cloned.1.call-start = ((), (), s32[]{:S(2)}) async-start(), calls=%async_computation.4 | async-start | bytes 6488064 | tf_op jit(solution)/shard_map/all_gather | solution.py:342
  13.0 189.8 %all-gather.14.cloned.1.call-start = ((), (), s32[]{:S(2)}) async-start(), calls=%async_computation.3 | async-start | bytes 6488064 | tf_op jit(solution)/shard_map/all_gather | solution.py:342
  15.2 248.8 %all-gather.12.cloned.1.call-start = ((), (), s32[]{:S(2)}) async-start(), calls=%async_computation.2 | async-start | bytes 6488064 | tf_op jit(solution)/shard_map/all_gather | solution.py:342
  16.8 35.4 %copy-start.89 = (f32[768]{0:T(1024)}, f32[768]{0:T(1024)S(1)}, u32[]{:S(2)}) copy-start(f32[768]{0:T(1024)S(1)} %get-tuple-element.120) | copy-start | bytes 9220
  19.6 98.7 %copy-start.32 = (f32[768,128]{1,0:T(8,128)}, f32[768,128]{1,0:T(8,128)S(1)}, u32[]{:S(2)}) copy-start(f32[768,128]{1,0:T(8,128)S(1)} %get-tuple-element.115) | copy-start | bytes 1179652
  20.4 27.4 %copy-start.2 = (bf16[768,2048]{1,0:T(8,128)(2,1)}, bf16[768,2048]{1,0:T(8,128)(2,1)S(1)}, u32[]{:S(2)}) copy-start(bf16[768,2048]{1,0:T(8,128)(2,1)S(1)} %fusion.2) | copy-start | bytes 9437188
  23.8 28.4 %copy-start.94 = (f32[32]{0:T(128)S(1)}, f32[32]{0:T(128)}, u32[]{:S(2)}) copy-start(f32[32]{0:T(128)} %copy-done.93) | copy-start | bytes 388
  53.0 2.1 collective-permute-start
  83.7 19.9 %collective-permute-start.9 = (bf16[192,2176]{1,0:T(8,128)(2,1)}, bf16[192,2176]{1,0:T(8,128)(2,1)S(1)}, u32[]{:S(2)}, u32[]{:S(2)}) collective-permute-start(bf16[192,2176]{1,0:T(8,128)(2,1)} %constant_dynamic-slice_fusion.7), channel_id=1, source_target_pairs={{0,2},{1,3},{2,0},{3,1},{4,6},{5,7},{6,4},{7,5},{8,10},{9,11},{10,... | collective-permute-start | bytes 2506760 | tf_op jit(solution)/shard_map/ppermute | solution.py:263
  85.9 547.2 %all-reduce.3.cloned.1.call-start = ((), (), s32[]{:S(2)}) async-start(), calls=%async_computation.7 | async-start | bytes 4653056 | tf_op jit(solution)/shard_map/psum | solution.py:568
  89.2 19.5 %collective-permute-start.1 = (bf16[192,2176]{1,0:T(8,128)(2,1)S(1)}, bf16[192,2176]{1,0:T(8,128)(2,1)S(1)}, u32[]{:S(2)}, u32[]{:S(2)}) collective-permute-start(bf16[192,2176]{1,0:T(8,128)(2,1)S(1)} %constant_dynamic-slice_fusion.10), channel_id=1, source_target_pairs={{0,1},{1,0},{2,3},{3,2},{4,5},{5,4},{6,7},{7,6},{8,9},{9,8},{10,11... | collective-permute-start | bytes 2506760 | tf_op jit(solution)/shard_map/ppermute | solution.py:263
  103.8 13.8 %collective-permute-start.10 = (bf16[96,2176]{1,0:T(8,128)(2,1)S(1)}, bf16[96,2176]{1,0:T(8,128)(2,1)S(1)}, u32[]{:S(2)}, u32[]{:S(2)}) collective-permute-start(bf16[96,2176]{1,0:T(8,128)(2,1)S(1)} %dynamic-slice_convert_fusion.5), channel_id=1, source_target_pairs={{0,1},{1,0},{2,3},{3,2},{4,5},{5,4},{6,7},{7,6},{8,9},{9,8},{10,11... | collective-permute-start | bytes 1253384 | tf_op jit(solution)/shard_map/ppermute | solution.py:267
  108.9 9.3 %collective-permute-start.2 = (bf16[96,2176]{1,0:T(8,128)(2,1)S(1)}, bf16[96,2176]{1,0:T(8,128)(2,1)S(1)}, u32[]{:S(2)}, u32[]{:S(2)}) collective-permute-start(bf16[96,2176]{1,0:T(8,128)(2,1)S(1)} %dynamic-slice_convert_fusion.7), channel_id=1, source_target_pairs={{0,2},{1,3},{2,0},{3,1},{4,6},{5,7},{6,4},{7,5},{8,10},{9,11},{10,... | collective-permute-start | bytes 1253384 | tf_op jit(solution)/shard_map/ppermute | solution.py:267
  121.0 10.1 %collective-permute-start.11 = (bf16[96,2176]{1,0:T(8,128)(2,1)S(1)}, bf16[96,2176]{1,0:T(8,128)(2,1)}, u32[]{:S(2)}, u32[]{:S(2)}) collective-permute-start(bf16[96,2176]{1,0:T(8,128)(2,1)S(1)} %pad_maximum_fusion.27), channel_id=1, source_target_pairs={{0,1},{1,0},{2,3},{3,2},{4,5},{5,4},{6,7},{7,6},{8,9},{9,8},{10,11... | collective-permute-start | bytes 1253384 | tf_op jit(solution)/shard_map/ppermute | solution.py:275
  123.2 10.5 %collective-permute-start.3 = (bf16[96,2176]{1,0:T(8,128)(2,1)}, bf16[96,2176]{1,0:T(8,128)(2,1)}, u32[]{:S(2)}, u32[]{:S(2)}) collective-permute-start(bf16[96,2176]{1,0:T(8,128)(2,1)} %pad_maximum_fusion.25), channel_id=1, source_target_pairs={{0,2},{1,3},{2,0},{3,1},{4,6},{5,7},{6,4},{7,5},{8,10},{9,11},{10,... | collective-permute-start | bytes 1253384 | tf_op jit(solution)/shard_map/ppermute | solution.py:275
  132.5 19.8 %collective-permute-start.12 = (bf16[192,2176]{1,0:T(8,128)(2,1)S(1)}, bf16[192,2176]{1,0:T(8,128)(2,1)}, u32[]{:S(2)}, u32[]{:S(2)}) collective-permute-start(bf16[192,2176]{1,0:T(8,128)(2,1)S(1)} %maximum_select_fusion.14), channel_id=1, source_target_pairs={{0,2},{1,3},{2,0},{3,1},{4,6},{5,7},{6,4},{7,5},{8,10},{9,11},{10,... | collective-permute-start | bytes 2506760 | tf_op jit(solution)/shard_map/ppermute | solution.py:279
  135.9 20.2 %collective-permute-start.4 = (bf16[192,2176]{1,0:T(8,128)(2,1)}, bf16[192,2176]{1,0:T(8,128)(2,1)}, u32[]{:S(2)}, u32[]{:S(2)}) collective-permute-start(bf16[192,2176]{1,0:T(8,128)(2,1)} %maximum_select_fusion.12), channel_id=1, source_target_pairs={{0,1},{1,0},{2,3},{3,2},{4,5},{5,4},{6,7},{7,6},{8,9},{9,8},{10,11... | collective-permute-start | bytes 2506760 | tf_op jit(solution)/shard_map/ppermute | solution.py:279
  154.6 109.4 %copy-start.17 = (bf16[384,2176]{1,0:T(8,128)(2,1)}, bf16[384,2176]{1,0:T(8,128)(2,1)S(1)}, u32[]{:S(2)}) copy-start(bf16[384,2176]{1,0:T(8,128)(2,1)S(1)} %maximum_select_fusion.6) | copy-start | bytes 5013508
  281.6 62.3 %collective-permute-start.21 = (bf16[192,2304]{1,0:T(8,128)(2,1)S(1)}, bf16[192,2304]{1,0:T(8,128)(2,1)S(1)}, u32[]{:S(2)}, u32[]{:S(2)}) collective-permute-start(bf16[192,2304]{1,0:T(8,128)(2,1)S(1)} %constant_dynamic-slice_fusion.4), channel_id=1, source_target_pairs={{0,2},{1,3},{2,0},{3,1},{4,6},{5,7},{6,4},{7,5},{8,10},{9,11},{10,... | collective-permute-start | bytes 2654216 | tf_op jit(solution)/shard_map/ppermute | solution.py:263
  301.6 44.0 %collective-permute-start.17 = (bf16[192,2304]{1,0:T(8,128)(2,1)S(1)}, bf16[192,2304]{1,0:T(8,128)(2,1)S(1)}, u32[]{:S(2)}, u32[]{:S(2)}) collective-permute-start(bf16[192,2304]{1,0:T(8,128)(2,1)S(1)} %constant_dynamic-slice_fusion.6), channel_id=1, source_target_pairs={{0,1},{1,0},{2,3},{3,2},{4,5},{5,4},{6,7},{7,6},{8,9},{9,8},{10,11... | collective-permute-start | bytes 2654216 | tf_op jit(solution)/shard_map/ppermute | solution.py:263
  306.4 20.5 %collective-permute-start.13 = (bf16[192,2176]{1,0:T(8,128)(2,1)S(1)}, bf16[192,2176]{1,0:T(8,128)(2,1)S(1)}, u32[]{:S(2)}, u32[]{:S(2)}) collective-permute-start(bf16[192,2176]{1,0:T(8,128)(2,1)S(1)} %fusion.65), channel_id=1, source_target_pairs={{0,2},{1,3},{2,0},{3,1},{4,6},{5,7},{6,4},{7,5},{8,10},{9,11},{10,... | collective-permute-start | bytes 2506760 | tf_op jit(solution)/shard_map/ppermute | solution.py:263
  311.1 31.0 %collective-permute-start.5 = (bf16[192,2176]{1,0:T(8,128)(2,1)S(1)}, bf16[192,2176]{1,0:T(8,128)(2,1)S(1)}, u32[]{:S(2)}, u32[]{:S(2)}) collective-permute-start(bf16[192,2176]{1,0:T(8,128)(2,1)S(1)} %fusion.67), channel_id=1, source_target_pairs={{0,1},{1,0},{2,3},{3,2},{4,5},{5,4},{6,7},{7,6},{8,9},{9,8},{10,11... | collective-permute-start | bytes 2506760 | tf_op jit(solution)/shard_map/ppermute | solution.py:263
  327.1 23.9 %collective-permute-start.14 = (bf16[96,2176]{1,0:T(8,128)(2,1)S(1)}, bf16[96,2176]{1,0:T(8,128)(2,1)S(1)}, u32[]{:S(2)}, u32[]{:S(2)}) collective-permute-start(bf16[96,2176]{1,0:T(8,128)(2,1)S(1)} %dynamic-slice_convert_fusion.4), channel_id=1, source_target_pairs={{0,1},{1,0},{2,3},{3,2},{4,5},{5,4},{6,7},{7,6},{8,9},{9,8},{10,11... | collective-permute-start | bytes 1253384 | tf_op jit(solution)/shard_map/ppermute | solution.py:267
  342.4 12.6 %collective-permute-start.6 = (bf16[96,2176]{1,0:T(8,128)(2,1)S(1)}, bf16[96,2176]{1,0:T(8,128)(2,1)S(1)}, u32[]{:S(2)}, u32[]{:S(2)}) collective-permute-start(bf16[96,2176]{1,0:T(8,128)(2,1)S(1)} %dynamic-slice_convert_fusion.6), channel_id=1, source_target_pairs={{0,2},{1,3},{2,0},{3,1},{4,6},{5,7},{6,4},{7,5},{8,10},{9,11},{10,... | collective-permute-start | bytes 1253384 | tf_op jit(solution)/shard_map/ppermute | solution.py:267
  344.1 15.7 %collective-permute-start.22 = (bf16[96,2304]{1,0:T(8,128)(2,1)S(1)}, bf16[96,2304]{1,0:T(8,128)(2,1)S(1)}, u32[]{:S(2)}, u32[]{:S(2)}) collective-permute-start(bf16[96,2304]{1,0:T(8,128)(2,1)S(1)} %dynamic-slice_convert_fusion.2), channel_id=1, source_target_pairs={{0,1},{1,0},{2,3},{3,2},{4,5},{5,4},{6,7},{7,6},{8,9},{9,8},{10,11... | collective-permute-start | bytes 1327112 | tf_op jit(solution)/shard_map/ppermute | solution.py:267
  345.9 16.3 %collective-permute-start.18 = (bf16[96,2304]{1,0:T(8,128)(2,1)S(1)}, bf16[96,2304]{1,0:T(8,128)(2,1)S(1)}, u32[]{:S(2)}, u32[]{:S(2)}) collective-permute-start(bf16[96,2304]{1,0:T(8,128)(2,1)S(1)} %dynamic-slice_convert_fusion.3), channel_id=1, source_target_pairs={{0,2},{1,3},{2,0},{3,1},{4,6},{5,7},{6,4},{7,5},{8,10},{9,11},{10,... | collective-permute-start | bytes 1327112 | tf_op jit(solution)/shard_map/ppermute | solution.py:267
  366.3 12.6 %collective-permute-start.15 = (bf16[96,2176]{1,0:T(8,128)(2,1)S(1)}, bf16[96,2176]{1,0:T(8,128)(2,1)S(1)}, u32[]{:S(2)}, u32[]{:S(2)}) collective-permute-start(bf16[96,2176]{1,0:T(8,128)(2,1)S(1)} %pad_maximum_fusion.28), channel_id=1, source_target_pairs={{0,1},{1,0},{2,3},{3,2},{4,5},{5,4},{6,7},{7,6},{8,9},{9,8},{10,11... | collective-permute-start | bytes 1253384 | tf_op jit(solution)/shard_map/ppermute | solution.py:275
  367.9 12.8 %collective-permute-start.19 = (bf16[96,2304]{1,0:T(8,128)(2,1)S(1)}, bf16[96,2304]{1,0:T(8,128)(2,1)S(1)}, u32[]{:S(2)}, u32[]{:S(2)}) collective-permute-start(bf16[96,2304]{1,0:T(8,128)(2,1)S(1)} %pad_maximum_fusion.23), channel_id=1, source_target_pairs={{0,2},{1,3},{2,0},{3,1},{4,6},{5,7},{6,4},{7,5},{8,10},{9,11},{10,... | collective-permute-start | bytes 1327112 | tf_op jit(solution)/shard_map/ppermute | solution.py:275
  369.5 19.0 %collective-permute-start.23 = (bf16[96,2304]{1,0:T(8,128)(2,1)S(1)}, bf16[96,2304]{1,0:T(8,128)(2,1)S(1)}, u32[]{:S(2)}, u32[]{:S(2)}) collective-permute-start(bf16[96,2304]{1,0:T(8,128)(2,1)S(1)} %pad_maximum_fusion.24), channel_id=1, source_target_pairs={{0,1},{1,0},{2,3},{3,2},{4,5},{5,4},{6,7},{7,6},{8,9},{9,8},{10,11... | collective-permute-start | bytes 1327112 | tf_op jit(solution)/shard_map/ppermute | solution.py:275
  379.1 21.6 %collective-permute-start.16 = (bf16[192,2176]{1,0:T(8,128)(2,1)S(1)}, bf16[192,2176]{1,0:T(8,128)(2,1)S(1)}, u32[]{:S(2)}, u32[]{:S(2)}) collective-permute-start(bf16[192,2176]{1,0:T(8,128)(2,1)S(1)} %maximum_select_fusion.15), channel_id=1, source_target_pairs={{0,2},{1,3},{2,0},{3,1},{4,6},{5,7},{6,4},{7,5},{8,10},{9,11},{10,... | collective-permute-start | bytes 2506760 | tf_op jit(solution)/shard_map/ppermute | solution.py:279
  380.8 23.7 %collective-permute-start.20 = (bf16[192,2304]{1,0:T(8,128)(2,1)S(1)}, bf16[192,2304]{1,0:T(8,128)(2,1)S(1)}, u32[]{:S(2)}, u32[]{:S(2)}) collective-permute-start(bf16[192,2304]{1,0:T(8,128)(2,1)S(1)} %maximum_select_fusion.10), channel_id=1, source_target_pairs={{0,1},{1,0},{2,3},{3,2},{4,5},{5,4},{6,7},{7,6},{8,9},{9,8},{10,11... | collective-permute-start | bytes 2654216 | tf_op jit(solution)/shard_map/ppermute | solution.py:279
  388.8 26.0 %collective-permute-start.24 = (bf16[192,2304]{1,0:T(8,128)(2,1)S(1)}, bf16[192,2304]{1,0:T(8,128)(2,1)S(1)}, u32[]{:S(2)}, u32[]{:S(2)}) collective-permute-start(bf16[192,2304]{1,0:T(8,128)(2,1)S(1)} %maximum_select_fusion.11), channel_id=1, source_target_pairs={{0,2},{1,3},{2,0},{3,1},{4,6},{5,7},{6,4},{7,5},{8,10},{9,11},{10,... | collective-permute-start | bytes 2654216 | tf_op jit(solution)/shard_map/ppermute | solution.py:279
  449.2 9.6 %collective-permute-start.25 = (f32[128,768]{1,0:T(8,128)S(1)}, f32[128,768]{1,0:T(8,128)S(1)}, u32[]{:S(2)}, u32[]{:S(2)}) collective-permute-start(f32[128,768]{1,0:T(8,128)S(1)} %constant_dynamic-slice_fusion.2), channel_id=1, source_target_pairs={{0,4},{4,0},{1,5},{5,1},{2,6},{6,2},{3,7},{7,3},{8,12},{12,8},{9,1... | collective-permute-start | bytes 1179656 | tf_op jit(solution)/shard_map/ppermute | solution.py:483
  462.4 22.7 %collective-permute-start.26 = (bf16[192,2432]{1,0:T(8,128)(2,1)S(1)}, bf16[192,2432]{1,0:T(8,128)(2,1)S(1)}, u32[]{:S(2)}, u32[]{:S(2)}) collective-permute-start(bf16[192,2432]{1,0:T(8,128)(2,1)S(1)} %constant_dynamic-slice_fusion.1), channel_id=1, source_target_pairs={{0,1},{1,0},{2,3},{3,2},{4,5},{5,4},{6,7},{7,6},{8,9},{9,8},{10,11... | collective-permute-start | bytes 2801672 | tf_op jit(solution)/shard_map/ppermute | solution.py:263
  464.4 22.7 %collective-permute-start.30 = (bf16[192,2432]{1,0:T(8,128)(2,1)S(1)}, bf16[192,2432]{1,0:T(8,128)(2,1)S(1)}, u32[]{:S(2)}, u32[]{:S(2)}) collective-permute-start(bf16[192,2432]{1,0:T(8,128)(2,1)S(1)} %constant_dynamic-slice_fusion), channel_id=1, source_target_pairs={{0,2},{1,3},{2,0},{3,1},{4,6},{5,7},{6,4},{7,5},{8,10},{9,11},{10,... | collective-permute-start | bytes 2801672 | tf_op jit(solution)/shard_map/ppermute | solution.py:263
  485.4 11.9 %collective-permute-start.27 = (bf16[96,2432]{1,0:T(8,128)(2,1)S(1)}, bf16[96,2432]{1,0:T(8,128)(2,1)S(1)}, u32[]{:S(2)}, u32[]{:S(2)}) collective-permute-start(bf16[96,2432]{1,0:T(8,128)(2,1)S(1)} %dynamic-slice_convert_fusion.1), channel_id=1, source_target_pairs={{0,2},{1,3},{2,0},{3,1},{4,6},{5,7},{6,4},{7,5},{8,10},{9,11},{10,... | collective-permute-start | bytes 1400840 | tf_op jit(solution)/shard_map/ppermute | solution.py:267
  487.4 11.9 %collective-permute-start.31 = (bf16[96,2432]{1,0:T(8,128)(2,1)S(1)}, bf16[96,2432]{1,0:T(8,128)(2,1)S(1)}, u32[]{:S(2)}, u32[]{:S(2)}) collective-permute-start(bf16[96,2432]{1,0:T(8,128)(2,1)S(1)} %dynamic-slice_convert_fusion), channel_id=1, source_target_pairs={{0,1},{1,0},{2,3},{3,2},{4,5},{5,4},{6,7},{7,6},{8,9},{9,8},{10,11... | collective-permute-start | bytes 1400840 | tf_op jit(solution)/shard_map/ppermute | solution.py:267
  504.5 12.6 %collective-permute-start.7 = (bf16[96,2176]{1,0:T(8,128)(2,1)S(1)}, bf16[96,2176]{1,0:T(8,128)(2,1)S(1)}, u32[]{:S(2)}, u32[]{:S(2)}) collective-permute-start(bf16[96,2176]{1,0:T(8,128)(2,1)S(1)} %pad_maximum_fusion.26), channel_id=1, source_target_pairs={{0,2},{1,3},{2,0},{3,1},{4,6},{5,7},{6,4},{7,5},{8,10},{9,11},{10,... | collective-permute-start | bytes 1253384 | tf_op jit(solution)/shard_map/ppermute | solution.py:275
  506.1 17.6 %collective-permute-start.28 = (bf16[96,2432]{1,0:T(8,128)(2,1)S(1)}, bf16[96,2432]{1,0:T(8,128)(2,1)S(1)}, u32[]{:S(2)}, u32[]{:S(2)}) collective-permute-start(bf16[96,2432]{1,0:T(8,128)(2,1)S(1)} %pad_maximum_fusion.21), channel_id=1, source_target_pairs={{0,2},{1,3},{2,0},{3,1},{4,6},{5,7},{6,4},{7,5},{8,10},{9,11},{10,... | collective-permute-start | bytes 1400840 | tf_op jit(solution)/shard_map/ppermute | solution.py:275
  507.4 19.1 %collective-permute-start.32 = (bf16[96,2432]{1,0:T(8,128)(2,1)S(1)}, bf16[96,2432]{1,0:T(8,128)(2,1)S(1)}, u32[]{:S(2)}, u32[]{:S(2)}) collective-permute-start(bf16[96,2432]{1,0:T(8,128)(2,1)S(1)} %pad_maximum_fusion.22), channel_id=1, source_target_pairs={{0,1},{1,0},{2,3},{3,2},{4,5},{5,4},{6,7},{7,6},{8,9},{9,8},{10,11... | collective-permute-start | bytes 1400840 | tf_op jit(solution)/shard_map/ppermute | solution.py:275
  517.3 21.6 %collective-permute-start.8 = (bf16[192,2176]{1,0:T(8,128)(2,1)S(1)}, bf16[192,2176]{1,0:T(8,128)(2,1)S(1)}, u32[]{:S(2)}, u32[]{:S(2)}) collective-permute-start(bf16[192,2176]{1,0:T(8,128)(2,1)S(1)} %maximum_select_fusion.13), channel_id=1, source_target_pairs={{0,1},{1,0},{2,3},{3,2},{4,5},{5,4},{6,7},{7,6},{8,9},{9,8},{10,11... | collective-permute-start | bytes 2506760 | tf_op jit(solution)/shard_map/ppermute | solution.py:279
  523.9 31.8 %collective-permute-start.29 = (bf16[192,2432]{1,0:T(8,128)(2,1)S(1)}, bf16[192,2432]{1,0:T(8,128)(2,1)S(1)}, u32[]{:S(2)}, u32[]{:S(2)}) collective-permute-start(bf16[192,2432]{1,0:T(8,128)(2,1)S(1)} %maximum_select_fusion.8), channel_id=1, source_target_pairs={{0,1},{1,0},{2,3},{3,2},{4,5},{5,4},{6,7},{7,6},{8,9},{9,8},{10,11... | collective-permute-start | bytes 2801672 | tf_op jit(solution)/shard_map/ppermute | solution.py:279
  526.6 29.8 %collective-permute-start.33 = (bf16[192,2432]{1,0:T(8,128)(2,1)S(1)}, bf16[192,2432]{1,0:T(8,128)(2,1)S(1)}, u32[]{:S(2)}, u32[]{:S(2)}) collective-permute-start(bf16[192,2432]{1,0:T(8,128)(2,1)S(1)} %maximum_select_fusion.9), channel_id=1, source_target_pairs={{0,2},{1,3},{2,0},{3,1},{4,6},{5,7},{6,4},{7,5},{8,10},{9,11},{10,... | collective-permute-start | bytes 2801672 | tf_op jit(solution)/shard_map/ppermute | solution.py:279
  556.3 84.1 %copy-start.7 = (bf16[384,2432]{1,0:T(8,128)(2,1)}, bf16[384,2432]{1,0:T(8,128)(2,1)S(1)}, u32[]{:S(2)}) copy-start(bf16[384,2432]{1,0:T(8,128)(2,1)S(1)} %maximum_select_fusion) | copy-start | bytes 5603332
  563.8 102.1 %all-gather.18.cloned.1.call-start = ((), (), s32[]{:S(2)}) async-start(), calls=%async_computation.5 | async-start | bytes 1966080 | tf_op jit(solution)/shard_map/all_gather | solution.py:569
  634.9 68.8 %all-gather.20.cloned.1.call-start = ((), (), s32[]{:S(2)}) async-start(), calls=%async_computation.6 | async-start | bytes 2621440 | tf_op jit(solution)/shard_map/all_gather | solution.py:553
  (115 other events, 465.2 us)
Sparse Core Ops, SparseCore 0:
  11.3 36.5 all-gather.7
  50.0 29.8 all-gather.9
  82.1 59.9 all-gather.15
  144.1 58.5 all-gather.13
  204.8 59.0 all-gather.11
  564.0 69.1 all-reduce.2
  635.5 30.4 all-gather.17
  668.4 35.2 all-gather.19
